TPU v7x, 512 devices: a whole 4x4x16 slice. The times are simulated.
512 devices in a mesh: feat: 64 (over x, z), dom: 8 (over y, core).
Axes of the slice: x: 4, y: 4, z: 16, core: 2. Of those that a mesh axis runs over, the one named last changes fastest.
Arguments:
- features: bfloat16 [65536, 1024], P('dom', 'feat'), may hold values from -6 to 6
- self_weight: bfloat16 [1024, 512], P('feat'), may hold values from -0.1875 to 0.1875
- neighbour_weight: bfloat16 [1024, 512], P('feat'), may hold values from -1.5 to 1.5
- cotangent: bfloat16 [65536, 512], P(('dom', 'feat')), may hold values from -0.09375 to 0.09375
- send_rows: int32 [8, 8, 256], replicated, may hold values from 0 to 8191
- send_count: int32 [8, 8], replicated, may hold values from 32 to 256, as said below
- tile_source: int32 [8, 64, 8], P('dom'), may hold values from 0 to 79
- tile_kind: int32 [8, 64, 8], P('dom'), may hold values from 0 to 63
- tile_patterns: bfloat16 [64, 128, 128], replicated, may hold values from 0.0099487305 to 1
Outputs:
- hidden: bfloat16 [65536, 512], P(('dom', 'feat'))
- grad_self: float32 [1024, 512], P('feat')
- grad_neighbour: float32 [1024, 512], P('feat')
Inputs may be any that keep to these rules, and one draw needn't show every extreme that they name: `send_count`: one destination has 256 live slots from every owner.
All inputs are finite; a program needn't handle non-finite values.
Results may differ from a plain program's by a relative error of at most 0.005.
Values may be sent and summed in bfloat16 or wider, within the bound.
A program may use at most 128 MiB of HBM per device.

v0:
```python
import jax
import jax.numpy as jnp
from jax import lax
from jax.sharding import PartitionSpec as P

inv_root_two = 0.7071067811865476
inv_root_two_pi = 0.3989422804014327


def gelu_pair(linear):
    normal_cdf = 0.5 * (1.0 + jax.scipy.special.erf(linear * inv_root_two))
    density = jnp.exp(-0.5 * linear * linear) * inv_root_two_pi
    return (linear * normal_cdf, normal_cdf + linear * density)


def on_device(
    features,
    self_weight,
    neighbour_weight,
    cotangent,
    send_rows,
    send_count,
    tile_source,
    tile_kind,
    tile_patterns,
):
    my_part = lax.axis_index("dom")
    part_count = lax.axis_size("dom")
    row_count = features.shape[0]
    col_count = features.shape[1]
    slot_count = send_rows.shape[2]
    tile_rows = tile_patterns.shape[1]
    slot_ids = jnp.arange(slot_count, dtype=jnp.int32)
    everything = lax.all_gather(features, "dom", axis=0, tiled=True)
    wanted = lax.dynamic_index_in_dim(send_rows, my_part, 1, keepdims=False)
    counts = lax.dynamic_index_in_dim(send_count, my_part, 1, keepdims=False)
    flat_ids = jnp.arange(part_count, dtype=jnp.int32)[:, None] * row_count + wanted
    remote = everything[flat_ids.reshape(-1)].reshape(part_count, slot_count, col_count)
    live_mask = slot_ids[None, :] < counts[:, None]
    remote = jnp.where(live_mask[:, :, None], remote, jnp.zeros((), jnp.bfloat16))
    extended = jnp.concatenate([features, remote.reshape(-1, col_count)], 0).reshape(
        -1, tile_rows, col_count
    )
    kinds = tile_kind[0]
    tile_mats = tile_patterns[kinds]
    sources = extended[tile_source[0]]
    summed = jnp.einsum("tkab,tkbf->taf", tile_mats, sources, preferred_element_type=jnp.float32)
    pattern_sums = jnp.sum(tile_patterns, axis=2, dtype=jnp.float32)
    degree = jnp.sum(pattern_sums[kinds], axis=1)
    neighbour_mean = (
        (summed / degree[:, :, None]).reshape(row_count, col_count).astype(jnp.bfloat16)
    )
    own_features, own_mean = (
        lax.all_to_all(features, "feat", split_axis=0, concat_axis=1, tiled=True),
        lax.all_to_all(neighbour_mean, "feat", split_axis=0, concat_axis=1, tiled=True),
    )
    linear = jnp.dot(
        own_features,
        lax.all_gather(self_weight, "feat", axis=0, tiled=True),
        preferred_element_type=jnp.float32,
    ) + jnp.dot(
        own_mean,
        lax.all_gather(neighbour_weight, "feat", axis=0, tiled=True),
        preferred_element_type=jnp.float32,
    )
    gelu_value, gelu_slope = gelu_pair(linear)
    hidden = gelu_value.astype(jnp.bfloat16)
    grad_linear = (cotangent.astype(jnp.float32) * gelu_slope).astype(jnp.bfloat16)
    shard_rows = lax.all_gather(grad_linear, "feat", axis=0, tiled=True)
    self_part = jnp.einsum("rc,rh->ch", features, shard_rows, preferred_element_type=jnp.float32)
    neigh_part = jnp.einsum(
        "rc,rh->ch", neighbour_mean, shard_rows, preferred_element_type=jnp.float32
    )
    self_local, neigh_local = (self_part, neigh_part)
    grad_self, grad_neighbour = lax.psum((self_local, neigh_local), "dom")
    return (hidden, grad_self, grad_neighbour)


def solution(mesh):
    placed = (
        P("dom", "feat"),
        P("feat", None),
        P("feat", None),
        P(("dom", "feat"), None),
        P(),
        P(),
        P("dom", None, None),
        P("dom", None, None),
        P(),
    )
    return jax.shard_map(
        on_device,
        mesh=mesh,
        in_specs=placed,
        out_specs=(P(("dom", "feat"), None), P("feat", None), P("feat", None)),
        check_vma=False,
    )
```

profile of v0, /device:TPU:1, one launch (start us, length us, event | category | flops | bytes accessed | tf_op | source)
XLA Modules:
  0.0 632.0 jit_solution(4560406625717011600)
XLA Ops:
  7.2 0.0 copy-start
  7.2 0.0 copy-start.1
  7.2 0.0 all-gather.7.cloned.1.call-start
  7.2 2.7 copy.29
  10.0 0.0 all-gather.7.cloned.1.call-update
  10.0 0.0 all-gather.5.cloned.1.call-start
  10.1 0.7 all-gather.5.cloned.1.call-update
  10.8 1.7 copy_bitcast_fusion.1
  12.5 19.1 %all-to-all-start = ((bf16[64,128,16]{1,2,0:T(8,128)(2,1)}), bf16[64,128,16]{1,2,0:T(8,128)(2,1)S(1)}, u32[]{:S(2)}, u32[]{:S(2)}) async-start(bf16[64,128,16]{1,2,0:T(8,128)(2,1)} %copy_bitcast_fusion.1), calls=%async_computation | async-start | bytes 524288 | tf_op jit(solution)/shard_map/all_to_all | solution.py:54
  31.6 0.0 all-gather.9.cloned.1.call-start
  31.6 0.7 all-gather.9.cloned.1.call-update
  32.3 0.1 broadcast_bitcast_fusion
  32.4 0.0 copy-done
  32.5 0.9 dynamic-slice_reduce_fusion
  33.3 0.1 iota_compare_fusion
  33.4 0.7 compare_select_fusion.1
  34.1 0.1 copy.31
  34.2 0.1 reshape.150
  34.3 0.7 compare_select_fusion.2
  35.0 0.1 copy.28
  35.1 0.1 reshape.134
  35.2 2.4 convert_reduce_fusion
  37.6 0.0 copy-done.1
  37.6 14.0 %gather_fusion = bf16[512,128,128]{2,1,0:T(8,128)(2,1)} fusion(bf16[64,128,128]{2,1,0:T(8,128)(2,1)S(1)} %copy-done.1, s32[1024]{0:T(1024)S(1)} %pad_clamp_fusion.1), kind=kCustom, calls=%fused_computation | custom fusion | bytes 33556480 | tf_op jit(solution)/shard_map/gather | solution.py:45
  51.6 0.0 copy-start.3
  51.6 1.0 gather_fusion.3
  52.6 0.1 bitcast_reduce_fusion
  52.7 55.8 %all-gather.7.cloned.1.call-done = bf16[65536,16]{1,0:T(8,128)(2,1)} async-done(((bf16[8192,16]{1,0:T(8,128)(2,1)}), bf16[65536,16]{1,0:T(8,128)(2,1)}) %all-gather.7.cloned.1.call-update) | async-done | bytes 2097168 | tf_op jit(solution)/shard_map/all_gather | solution.py:34
  108.5 13.5 %gather_fusion.1 = bf16[2048,16]{1,0:T(8,128)(2,1)S(1)} fusion(bf16[65536,16]{1,0:T(8,128)(2,1)} %all-gather.7.cloned.1.call-done, s32[2048]{0:T(1024)S(1)} %broadcast_clamp_fusion), kind=kCustom, calls=%fused_computation.1 | custom fusion | bytes 139264 | tf_op jit(solution)/shard_map/gather | solution.py:38
  122.0 0.3 broadcast_select_fusion
  122.4 0.2 copy.30
  122.5 0.0 copy-done.3
  122.5 0.1 copy_bitcast_fusion
  122.6 2.0 gather_fusion.2
  124.6 0.0 copy-start.4
  124.7 8.9 %fusion.1 = bf16[64,128,16]{1,2,0:T(8,128)(2,1)} fusion(bf16[64,8,128,128]{3,2,1,0:T(8,128)(2,1)} %bitcast.61, bf16[64,8,128,16]{2,3,1,0:T(8,128)(2,1)S(1)} %bitcast.60, f32[64,128]{1,0:T(8,128)S(1)} %bitcast_reduce_fusion), kind=kOutput, calls=%fused_computation.9 | convolution fusion | flops 268697600 | bytes 19169280 | tf_op jit(solution)/shard_map/tkab,tkbf->taf/dot_general | solution.py:47
  133.5 0.0 all-to-all-done
  133.5 15.3 %all-to-all-start.1 = ((bf16[64,128,16]{1,2,0:T(8,128)(2,1)}), bf16[64,128,16]{1,2,0:T(8,128)(2,1)S(1)}, u32[]{:S(2)}, u32[]{:S(2)}) async-start(bf16[64,128,16]{1,2,0:T(8,128)(2,1)} %fusion.1), calls=%async_computation.1 | async-start | bytes 524288 | tf_op jit(solution)/shard_map/all_to_all | solution.py:55
  148.9 0.0 all-gather.11.cloned.1.call-start
  148.9 93.0 %all-gather.5.cloned.1.call-done = bf16[1024,512]{1,0:T(8,128)(2,1)} async-done(((bf16[16,512]{1,0:T(8,128)(2,1)}), bf16[1024,512]{1,0:T(8,128)(2,1)}) %all-gather.5.cloned.1.call-update) | async-done | bytes 1048592 | tf_op jit(solution)/shard_map/all_gather | solution.py:59
  241.9 1.5 fusion.11
  243.4 137.4 %all-gather.9.cloned.1.call-done = bf16[1024,512]{1,0:T(8,128)(2,1)} async-done(((bf16[16,512]{1,0:T(8,128)(2,1)}), bf16[1024,512]{1,0:T(8,128)(2,1)}) %all-gather.9.cloned.1.call-update) | async-done | bytes 1048592 | tf_op jit(solution)/shard_map/all_gather | solution.py:63
  380.8 0.0 all-to-all-done.1
  380.8 0.0 copy-done.4
  380.8 2.4 fusion.7
  383.2 0.0 all-gather.11.cloned.1.call-update
  383.2 0.0 all-reduce.3.cloned.1.call-start
  383.3 154.9 %all-gather.11.cloned.1.call-done = bf16[8192,512]{1,0:T(8,128)(2,1)} async-done(((bf16[128,512]{1,0:T(8,128)(2,1)}), bf16[8192,512]{1,0:T(8,128)(2,1)}) %all-gather.11.cloned.1.call-update) | async-done | bytes 8388624 | tf_op jit(solution)/shard_map/all_gather | solution.py:69
  538.2 0.0 copy-start.2
  538.2 5.4 fusion.8
  543.6 0.4 copy-done.2
  544.0 1.8 convolution_bitcast_fusion.1
  545.8 0.0 all-reduce.3.cloned.1.call-update
  545.9 76.9 %all-reduce.3.cloned.1.call-done = (f32[16,512]{1,0:T(8,128)}, f32[16,512]{1,0:T(8,128)}) async-done(((f32[16,512]{1,0:T(8,128)}, f32[16,512]{1,0:T(8,128)}), (f32[16,512]{1,0:T(8,128)}, f32[16,512]{1,0:T(8,128)})) %all-reduce.3.cloned.1.call-update) | async-done | bytes 65552 | tf_op jit(solution)/shard_map/psum | solution.py:75
  622.8 1.4 copy.47
  624.1 1.4 copy.48
  (8 shorter events, 0.1 us)
Async XLA Ops:
  7.2 25.2 %copy-start = (s32[8,8,256]{2,1,0:T(8,128)S(1)}, s32[8,8,256]{2,1,0:T(8,128)}, u32[]{:S(2)}) copy-start(s32[8,8,256]{2,1,0:T(8,128)} %param.13) | copy-start | bytes 196612
  7.2 30.4 %copy-start.1 = (bf16[64,128,128]{2,1,0:T(8,128)(2,1)S(1)}, bf16[64,128,128]{2,1,0:T(8,128)(2,1)}, u32[]{:S(2)}) copy-start(bf16[64,128,128]{2,1,0:T(8,128)(2,1)} %param.17) | copy-start | bytes 6291460
  7.2 101.3 %all-gather.7.cloned.1.call-start = ((), (), s32[]{:S(2)}) async-start(), calls=%async_computation.3 | async-start | bytes 18874368 | tf_op jit(solution)/shard_map/all_gather | solution.py:34
  10.0 231.9 %all-gather.5.cloned.1.call-start = ((), (), s32[]{:S(2)}) async-start(), calls=%async_computation.2 | async-start | bytes 1064960 | tf_op jit(solution)/shard_map/all_gather | solution.py:59
  12.5 121.1 %all-to-all-start = ((bf16[64,128,16]{1,2,0:T(8,128)(2,1)}), bf16[64,128,16]{1,2,0:T(8,128)(2,1)S(1)}, u32[]{:S(2)}, u32[]{:S(2)}) async-start(bf16[64,128,16]{1,2,0:T(8,128)(2,1)} %copy_bitcast_fusion.1), calls=%async_computation | async-start | bytes 524288 | tf_op jit(solution)/shard_map/all_to_all | solution.py:54
  31.6 349.3 %all-gather.9.cloned.1.call-start = ((), (), s32[]{:S(2)}) async-start(), calls=%async_computation.4 | async-start | bytes 1064960 | tf_op jit(solution)/shard_map/all_gather | solution.py:63
  51.6 70.9 %copy-start.3 = (bf16[8192,16]{0,1:T(8,128)(2,1)S(1)}, bf16[8192,16]{0,1:T(8,128)(2,1)}, u32[]{:S(2)}) copy-start(bf16[8192,16]{0,1:T(8,128)(2,1)} %param.9) | copy-start | bytes 786436
  124.6 256.2 %copy-start.4 = (bf16[128,512]{1,0:T(8,128)(2,1)S(1)}, bf16[128,512]{1,0:T(8,128)(2,1)}, u32[]{:S(2)}) copy-start(bf16[128,512]{1,0:T(8,128)(2,1)} %param.12) | copy-start | bytes 393220
  133.5 247.3 %all-to-all-start.1 = ((bf16[64,128,16]{1,2,0:T(8,128)(2,1)}), bf16[64,128,16]{1,2,0:T(8,128)(2,1)S(1)}, u32[]{:S(2)}, u32[]{:S(2)}) async-start(bf16[64,128,16]{1,2,0:T(8,128)(2,1)} %fusion.1), calls=%async_computation.1 | async-start | bytes 524288 | tf_op jit(solution)/shard_map/all_to_all | solution.py:55
  148.9 389.3 %all-gather.11.cloned.1.call-start = ((), (), s32[]{:S(2)}) async-start(), calls=%async_computation.5 | async-start | bytes 8519680 | tf_op jit(solution)/shard_map/all_gather | solution.py:69
  383.2 239.6 %all-reduce.3.cloned.1.call-start = ((), (), s32[]{:S(2)}) async-start(), calls=%async_computation.6 | async-start | bytes 131072 | tf_op jit(solution)/shard_map/psum | solution.py:75
  538.2 5.9 copy-start.2
Sparse Core Ops, SparseCore 0:
  10.2 98.2 all-gather.6
  111.4 130.4 all-gather.4
  244.8 135.9 all-gather.8
  383.6 154.4 all-gather.10
  546.0 76.7 all-reduce.2
where the time goes:
time: 633 us; the launch traced here: 632 us
  waiting for transfers between devices  519 us (82%)
  local copies, waits for them, and re-layouts  39.7 us (6%)
  starting transfers between devices  34.6 us (5%)
  matrix products  20 us (3%)
  between operations  13.9 us (2%)
    all_gather x1, waiting for transfers between devices, on_device(): shard_rows = lax.all_gather(grad_linear, 'feat', axis=0, tiled=True)  155 us
    all_gather x1, waiting for transfers between devices, on_device(): lax.all_gather(neighbour_weight, 'feat', axis=0, tiled=True)  137 us
    all_gather x1, waiting for transfers between devices, on_device(): lax.all_gather(self_weight, 'feat', axis=0, tiled=True)  93 us
    psum x1, waiting for transfers between devices, on_device(): grad_self, grad_neighbour = lax.psum((self_local, neigh_local), 'dom')  76.9 us
    all_gather x1, waiting for transfers between devices, on_device(): everything = lax.all_gather(features, 'dom', axis=0, tiled=True)  55.8 us
    all_to_all x1, starting transfers between devices, on_device(): lax.all_to_all(features, 'feat', split_axis=0, concat_axis=1, tiled=True)  19.1 us
    all_to_all x1, starting transfers between devices, on_device(): lax.all_to_all(neighbour_mean, 'feat', split_axis=0, concat_axis=1, tiled...  15.3 us
    gather x1, local copies, waits for them, and re-layouts, on_device(): tile_mats = tile_patterns[kinds]  14 us
  transfers between devices with their start and end apart: 7, of which 5 were waited for; matrix products, arithmetic and copies ran while one was open for 8% of the time, Pallas kernels for 0%

commit v1 on v0

v1 whole, which is shorter than its diff:
```python
import jax
import jax.numpy as jnp
from jax import lax
from jax.experimental import pallas as pl
from jax.experimental.pallas import tpu as pltpu
from jax.sharding import PartitionSpec as P

FEAT_GRID = (4, 16)
DOM_GRID = (4, 2)
inv_root_two = 0.7071067811865476
inv_root_two_pi = 0.3989422804014327
BF = jnp.bfloat16
F32 = jnp.float32
MESH = pl.DeviceIdType.MESH


def gelu_pair(linear):
    normal_cdf = 0.5 * (1.0 + lax.erf(linear * inv_root_two))
    density = jnp.exp(-0.5 * linear * linear) * inv_root_two_pi
    return linear * normal_cdf, normal_cdf + linear * density


def drain(ref, sem):
    pltpu.make_async_copy(ref, ref, sem).wait()


def layer(
    x_ref, w1_ref, w2_ref, cot_ref, rows_ref, pat_ref, count_ref, source_ref, kind_ref,
    hid_ref, gs_ref, gn_ref,
    ext, halo_out, mean, xm, weights, grad, other, other_in, part, part_in, kept,
    column, column_in, cell, cell_in, final,
    sem_out, sem_in, core_sem, y_sem,
):
    nx, nz = FEAT_GRID
    ny, nc = DOM_GRID
    nf, nd = nx * nz, ny * nc
    feat = lax.axis_index("feat")
    dom = lax.axis_index("dom")
    x, z = feat // nz, feat % nz
    y, core = dom // nc, dom % nc
    width = x_ref.shape[0]
    depth = nf * width
    band = nz * width
    tiles = nf
    slot_tiles = halo_out.shape[1]
    slots = rows_ref.shape[2]
    steps = source_ref.shape[0]

    def send(src, dst, phase, where, recv=None):
        pltpu.make_async_remote_copy(
            src_ref=src, dst_ref=dst, send_sem=sem_out.at[phase],
            recv_sem=sem_in.at[phase] if recv is None else recv,
            device_id=where, device_id_type=MESH,
        ).start()

    def feat_at(fx, fz):
        return {"feat": fx * nz + fz, "dom": dom}

    def dom_at(dy, dc):
        return {"feat": feat, "dom": dy * nc + dc}

    barrier = pltpu.get_barrier_semaphore()

    def greet_feat(i, _):
        pl.semaphore_signal(
            barrier, inc=1, device_id={"feat": (feat + i) % nf, "dom": dom}, device_id_type=MESH
        )
        return 0

    def greet_dom(i, _):
        pl.semaphore_signal(
            barrier, inc=1, device_id={"feat": feat, "dom": (dom + i) % nd}, device_id_type=MESH
        )
        return 0

    lax.fori_loop(1, nf, greet_feat, 0)
    lax.fori_loop(1, nd, greet_dom, 0)

    def take(t, _):
        ext[t] = x_ref[:, pl.ds(pl.multiple_of(t * 128, 128), 128)]
        return 0

    lax.fori_loop(0, tiles, take, 0)
    xm[0, feat] = ext[feat]
    block = pl.ds(pl.multiple_of(y * 128, 128), 128)
    weights[core, y, x, z] = jnp.where(core == 0, w1_ref[:, block], w2_ref[:, block])
    pl.semaphore_wait(barrier, nf - 1 + nd - 1)

    def weights_z(i, _):
        there = weights.at[core, y, x, z]
        send(there, there, 0, feat_at(x, (z + i) % nz))
        return 0

    lax.fori_loop(1, nz, weights_z, 0)

    def features_out(i, _):
        peer = (feat + i) % nf
        send(ext.at[peer], xm.at[0, feat], 1, {"feat": peer, "dom": dom})
        return 0

    lax.fori_loop(1, nf, features_out, 0)

    group = min(tiles, 16)
    lane_ids = lax.broadcasted_iota(jnp.int32, (128, slots), 0)
    slot_ids = lax.broadcasted_iota(jnp.int32, (1, slots), 1)

    def pick(dest):
        wanted = rows_ref[dom, pl.ds(dest, 1), :]
        low, high = wanted & 127, wanted >> 7
        choose = jnp.where(lane_ids == low, 1.0, 0.0).astype(BF)
        found = jnp.zeros((width, slots), F32)
        for g in range(0, tiles, group):
            rows = ext[g : g + group].reshape(group * width, 128)
            spread = jnp.dot(rows, choose, preferred_element_type=F32)
            for h in range(group):
                found = jnp.where(
                    high == g + h, spread[h * width : (h + 1) * width], found
                )
        live = slot_ids < count_ref[dom, dest]
        return jnp.where(live, found, 0.0).astype(BF)

    def halo_send(i, _):
        dest = (dom + i) % nd
        found = pick(dest)
        for j in range(slot_tiles):
            halo_out[dest, j] = found[:, j * 128 : (j + 1) * 128]
        send(
            halo_out.at[dest], ext.at[pl.ds(tiles + dom * slot_tiles, slot_tiles)], 2,
            {"feat": feat, "dom": dest},
        )
        return 0

    lax.fori_loop(1, nd, halo_send, 0)
    found = pick(dom)
    for j in range(slot_tiles):
        ext[tiles + dom * slot_tiles + j] = found[:, j * 128 : (j + 1) * 128]

    drain(weights.at[core, y, x, pl.ds(0, nz - 1)], sem_in.at[0])

    def weights_x(i, _):
        there = weights.at[core, y, x]
        send(there, there, 3, feat_at((x + i) % nx, z))
        return 0

    lax.fori_loop(1, nx, weights_x, 0)
    drain(ext.at[pl.ds(tiles, (nd - 1) * slot_tiles)], sem_in.at[2])
    drain(weights.at[core, y, pl.ds(0, nx - 1)], sem_in.at[3])

    def weights_y(i, _):
        there = weights.at[core, y]
        send(there, there, 4, dom_at((y + i) % ny, core))
        return 0

    lax.fori_loop(1, ny, weights_y, 0)

    ones = jnp.ones((width, 256), BF)

    def mean_of(t):
        total = jnp.zeros((2 * width, 128), F32)
        for k in range(0, steps, 2):
            left = jnp.concatenate([ext[source_ref[k, t]], ext[source_ref[k + 1, t]]], axis=1)
            right = jnp.concatenate([pat_ref[kind_ref[k, t]], pat_ref[kind_ref[k + 1, t]]], axis=1)
            total = total + lax.dot_general(
                jnp.concatenate([left, ones], axis=0), right, (((1,), (1,)), ((), ())),
                preferred_element_type=F32,
            )
        return (total[:width] / total[width : width + 1]).astype(BF)

    def mean_out(i, _):
        peer = (feat + i) % nf
        mean[peer] = mean_of(peer)
        send(mean.at[peer], xm.at[1, feat], 5, {"feat": peer, "dom": dom})
        return 0

    lax.fori_loop(1, nf, mean_out, 0)
    xm[1, feat] = mean_of(feat)

    drain(weights.at[core, pl.ds(0, ny - 1)], sem_in.at[4])
    send(weights.at[core], weights.at[core], 6, dom_at(y, 1 - core))
    drain(xm.at[0, pl.ds(0, nf - 1)], sem_in.at[1])
    drain(weights.at[core], sem_in.at[6])
    drain(xm.at[1, pl.ds(0, nf - 1)], sem_in.at[5])

    own = [xm[m].reshape(depth, 128) for m in range(2)]
    for b in range(ny):
        span = slice(b * 128, (b + 1) * 128)
        linear = jnp.zeros((128, 128), F32)
        for m in range(2):
            linear = linear + lax.dot_general(
                own[m], weights[m, b].reshape(depth, 128), (((0,), (0,)), ((), ())),
                preferred_element_type=F32,
            )
        value, slope = gelu_pair(linear)
        hid_ref[:, span] = value.astype(BF)
        grad[:, span] = (cot_ref[:, span].astype(F32) * slope).astype(BF)

    def product(m, b):
        return jnp.dot(
            xm[m, pl.ds(b * nz, nz)].reshape(band, 128), grad[...], preferred_element_type=F32
        )

    def core_out(i, _):
        b = (x + i) % nx
        result = product(1 - core, b).astype(BF)
        for c in range(ny):
            other[b, c] = result[:, c * 128 : (c + 1) * 128]
        send(other.at[b], other_in.at[b], 7, dom_at(y, 1 - core), core_sem.at[b])
        return 0

    lax.fori_loop(1, nx + 1, core_out, 0)

    def y_out(i, _):
        b = (x + i) % nx
        result = product(core, b)
        drain(other_in.at[b], core_sem.at[b])
        for c in range(ny):
            summed = result[:, c * 128 : (c + 1) * 128] + other_in[b, c].astype(F32)
            part[b, c] = summed.astype(BF)

            @pl.when(c == y)
            def _():
                kept[b] = summed

        def one(j, _):
            c = (y + j) % ny
            send(part.at[b, c], part_in.at[b, y], 8, dom_at(c, core), y_sem.at[b])
            return 0

        lax.fori_loop(1, ny, one, 0)
        return 0

    lax.fori_loop(1, nx + 1, y_out, 0)

    def y_sum(b):
        drain(part_in.at[b, pl.ds(0, ny - 1)], y_sem.at[b])
        total = kept[b]
        for j in range(1, ny):
            total = total + part_in[b, (y + j) % ny].astype(F32)
        return total

    def x_out(i, _):
        b = (x + i) % nx
        column[b] = y_sum(b).astype(BF)
        send(column.at[b], column_in.at[x], 9, feat_at(b, z))
        return 0

    lax.fori_loop(1, nx, x_out, 0)
    total = y_sum(x)
    drain(column_in.at[pl.ds(0, nx - 1)], sem_in.at[9])
    for j in range(1, nx):
        total = total + column_in[(x + j) % nx].astype(F32)

    kept[x] = total
    cell[...] = total.astype(BF).reshape(nz, width, 128)

    def z_out(i, _):
        peer = (z + i) % nz
        send(cell.at[peer], cell_in.at[z], 10, feat_at(x, peer))
        return 0

    lax.fori_loop(1, nz, z_out, 0)
    drain(cell_in.at[pl.ds(0, nz - 1)], sem_in.at[10])
    total = kept[x, pl.ds(pl.multiple_of(z * width, width), width)]
    for j in range(1, nz):
        total = total + cell_in[(z + j) % nz].astype(F32)

    final[dom] = total

    def dom_out(i, _):
        send(final.at[dom], final.at[dom], 11, {"feat": feat, "dom": (dom + i) % nd})
        return 0

    lax.fori_loop(1, nd, dom_out, 0)
    drain(final.at[pl.ds(0, nd - 1)], sem_in.at[11])
    for b in range(ny):
        span = slice(b * 128, (b + 1) * 128)
        gs_ref[:, span] = final[b * nc]
        gn_ref[:, span] = final[b * nc + 1]

    drain(weights.at[core, y, x, pl.ds(0, nz - 1)], sem_out.at[0])
    drain(ext.at[pl.ds(0, nf - 1)], sem_out.at[1])
    drain(halo_out.at[pl.ds(0, nd - 1)], sem_out.at[2])
    drain(weights.at[core, y, pl.ds(0, nx - 1)], sem_out.at[3])
    drain(weights.at[core, pl.ds(0, ny - 1)], sem_out.at[4])
    drain(mean.at[pl.ds(0, nf - 1)], sem_out.at[5])
    drain(weights.at[core], sem_out.at[6])
    drain(other, sem_out.at[7])
    drain(part.at[:, pl.ds(0, ny - 1)], sem_out.at[8])
    drain(column.at[pl.ds(0, nx - 1)], sem_out.at[9])
    drain(cell.at[pl.ds(0, nz - 1)], sem_out.at[10])
    drain(final.at[pl.ds(0, nd - 1)], sem_out.at[11])


def on_device(features, w1, w2, cotangent, send_rows, send_count, tile_source, tile_kind, patterns):
    nx, nz = FEAT_GRID
    ny, nc = DOM_GRID
    nf, nd = nx * nz, ny * nc
    width = features.shape[1]
    hidden = w1.shape[1]
    slot_tiles = send_rows.shape[2] // 128
    assert features.shape[0] == nf * 128 and hidden == ny * 128 and nc == 2
    band = nz * width
    vmem = pl.BlockSpec(memory_space=pltpu.VMEM)
    smem = pl.BlockSpec(memory_space=pltpu.SMEM)
    return pl.pallas_call(
        layer,
        out_shape=(
            jax.ShapeDtypeStruct((128, hidden), BF),
            jax.ShapeDtypeStruct((width, hidden), F32),
            jax.ShapeDtypeStruct((width, hidden), F32),
        ),
        in_specs=[vmem] * 6 + [smem] * 3,
        out_specs=(vmem,) * 3,
        scratch_shapes=[
            pltpu.VMEM((nf + nd * slot_tiles, width, 128), BF),
            pltpu.VMEM((nd, slot_tiles, width, 128), BF),
            pltpu.VMEM((nf, width, 128), BF),
            pltpu.VMEM((2, nf, width, 128), BF),
            pltpu.VMEM((nc, ny, nx, nz, width, 128), BF),
            pltpu.VMEM((128, hidden), BF),
            pltpu.VMEM((nx, ny, band, 128), BF),
            pltpu.VMEM((nx, ny, band, 128), BF),
            pltpu.VMEM((nx, ny, band, 128), BF),
            pltpu.VMEM((nx, ny, band, 128), BF),
            pltpu.VMEM((nx, band, 128), F32),
            pltpu.VMEM((nx, band, 128), BF),
            pltpu.VMEM((nx, band, 128), BF),
            pltpu.VMEM((nz, width, 128), BF),
            pltpu.VMEM((nz, width, 128), BF),
            pltpu.VMEM((nd, width, 128), F32),
            pltpu.SemaphoreType.DMA((12,)),
            pltpu.SemaphoreType.DMA((12,)),
            pltpu.SemaphoreType.DMA((nx,)),
            pltpu.SemaphoreType.DMA((nx,)),
        ],
        compiler_params=pltpu.CompilerParams(
            collective_id=0, has_side_effects=True, vmem_limit_bytes=48 << 20
        ),
    )(
        features.T, w1, w2, cotangent, send_rows, patterns, send_count,
        tile_source[0].T, tile_kind[0].T,
    )


def solution(mesh):
    placed = (
        P("dom", "feat"),
        P("feat", None),
        P("feat", None),
        P(("dom", "feat"), None),
        P(),
        P(),
        P("dom", None, None),
        P("dom", None, None),
        P(),
    )
    return jax.shard_map(
        on_device,
        mesh=mesh,
        in_specs=placed,
        out_specs=(P(("dom", "feat"), None), P("feat", None), P("feat", None)),
        check_vma=False,
    )
```

time: 633 us -> 92 us (0.15)
  waiting for transfers between devices: 519 us -> 0 us
  Pallas kernels: 0 us -> 81.3 us
  starting transfers between devices: 34.6 us -> 0 us
  local copies, waits for them, and re-layouts: 39.7 us -> 9.66 us
  matrix products: 20 us -> 0 us
  between operations: 13.9 us -> 0.66 us
    all_gather x4 -> x0, waiting for transfers between devices: 441 us -> none  [the longest x1 155 us: on_device(): shard_rows = lax.all_gather(grad_linear, 'feat', axis=0, tiled=True)]
    pallas_call x0 -> x1, Pallas kernels: none -> 81.3 us  [on_device(): pl.pallas_call(layer, out_shape=(jax.ShapeDtypeStruct((128, hidden), BF),...]
    psum x1 -> x0, waiting for transfers between devices: 76.9 us -> none  [on_device(): grad_self, grad_neighbour = lax.psum((self_local, neigh_local), 'dom')]
    all_to_all x2 -> x0, starting transfers between devices: 34.4 us -> none  [the longest x1 19.1 us: on_device(): lax.all_to_all(features, 'feat', split_axis=0, concat_axis=1, tiled=True)]
    gather x4 -> x0, local copies, waits for them, and re-layouts: 30.6 us -> none  [the longest x1 14 us: on_device(): tile_mats = tile_patterns[kinds]]
    dot_general x5 -> x0, matrix products: 20 us -> none  [the longest x1 8.87 us: on_device(): jnp.einsum('tkab,tkbf->taf', tile_mats, sources, preferred_element_type=j...]
  transfers between devices with their start and end apart: 7 -> 0, of which waited for: 5 -> 0; matrix products, arithmetic and copies ran while one was open for 8% -> 0% of each run, Pallas kernels for 0% -> 0%
where the time goes in v1:
time: 92 us; the launch traced here: 91.6 us
  Pallas kernels  81.3 us (88%)
  local copies, waits for them, and re-layouts  9.66 us (10%)
    pallas_call x1, Pallas kernels, on_device(): pl.pallas_call(layer, out_shape=(jax.ShapeDtypeStruct((128, hidden), BF),...  81.3 us
    unnamed x21, local copies, waits for them, and re-layouts  9.66 us

profile of v1, /device:TPU:1, one launch (start us, length us, event | category | flops | bytes accessed | tf_op | source)
XLA Modules:
  0.0 91.6 jit_solution(13290865948387572513)
XLA Ops:
  0.6 0.0 copy-start
  0.6 1.6 %copy-done = bf16[64,128,128]{2,1,0:T(8,128)(2,1)S(1)} copy-done((bf16[64,128,128]{2,1,0:T(8,128)(2,1)S(1)}, bf16[64,128,128]{2,1,0:T(8,128)(2,1)}, u32[]{:S(2)}) %copy-start) | copy-done | bytes 2097176
  2.2 0.0 copy-start.1
  2.2 0.9 %copy-done.1 = bf16[8192,16]{0,1:T(8,128)(2,1)S(1)} copy-done((bf16[8192,16]{0,1:T(8,128)(2,1)S(1)}, bf16[8192,16]{0,1:T(8,128)(2,1)}, u32[]{:S(2)}) %copy-start.1) | copy-done | bytes 262168
  3.2 0.0 copy-start.2
  3.2 0.9 copy-done.2
  4.1 0.0 copy-start.3
  4.1 0.8 copy-done.3
  4.9 0.0 copy-start.4
  4.9 0.7 copy-done.4
  5.6 0.0 copy-start.5
  5.6 0.7 copy-done.5
  6.4 0.0 copy-start.6
  6.4 0.7 copy-done.6
  7.0 0.0 copy-start.7
  7.0 0.7 copy-done.7
  7.7 0.0 copy-start.8
  7.7 0.7 copy-done.8
  8.4 81.3 %shard_map.112 = (bf16[128,512]{1,0:T(8,128)(2,1)S(1)}, f32[16,512]{1,0:T(8,128)S(1)}, f32[16,512]{1,0:T(8,128)S(1)}) custom-call(bf16[16,8192]{1,0:T(8,128)(2,1)S(1)} %bitcast.7, bf16[16,512]{1,0:T(8,128)(2,1)S(1)} %copy-done.4, bf16[16,512]{1,0:T(8,128)(2,1)S(1)} %copy-done.5, bf16[128,512]{1,0:T(8,128)(2,1)S(1)} %copy-done.2, s32[8,8,256]{2,1,0:T(8,128)S(1)} %copy-done.3, ...), custom_call_target="tpu_custom_call" | custom-call | tf_op jit(solution)/shard_map/pallas_call | solution.py:305
  89.7 0.7 copy.15
  90.3 0.6 copy.16
  91.0 0.6 copy.17
Async XLA Ops:
  0.6 1.6 %copy-start = (bf16[64,128,128]{2,1,0:T(8,128)(2,1)S(1)}, bf16[64,128,128]{2,1,0:T(8,128)(2,1)}, u32[]{:S(2)}) copy-start(bf16[64,128,128]{2,1,0:T(8,128)(2,1)} %pat_ref.1) | copy-start | bytes 6291460
  2.2 0.9 %copy-start.1 = (bf16[8192,16]{0,1:T(8,128)(2,1)S(1)}, bf16[8192,16]{0,1:T(8,128)(2,1)}, u32[]{:S(2)}) copy-start(bf16[8192,16]{0,1:T(8,128)(2,1)} %param.9) | copy-start | bytes 786436
  3.2 0.9 copy-start.2
  4.1 0.8 copy-start.3
  4.9 0.7 copy-start.4
  5.6 0.7 copy-start.5
  6.4 0.7 copy-start.6
  7.0 0.7 copy-start.7
  7.7 0.7 copy-start.8

commit v2 on v1

v2 whole, which is shorter than its diff:
```python
import jax
import jax.numpy as jnp
from jax import lax
from jax.experimental import pallas as pl
from jax.experimental.pallas import tpu as pltpu
from jax.sharding import PartitionSpec as P

FEAT_GRID = (4, 16)
DOM_GRID = (4, 2)
inv_root_two = 0.7071067811865476
inv_root_two_pi = 0.3989422804014327
BF = jnp.bfloat16
F32 = jnp.float32
MESH = pl.DeviceIdType.MESH


def gelu_pair(linear):
    normal_cdf = 0.5 * (1.0 + lax.erf(linear * inv_root_two))
    density = jnp.exp(-0.5 * linear * linear) * inv_root_two_pi
    return linear * normal_cdf, normal_cdf + linear * density


def drain(ref, sem):
    pltpu.make_async_copy(ref, ref, sem).wait()


def layer(
    x_hbm, w1_hbm, w2_hbm, cot_hbm, rows_hbm, pat_hbm, count_hbm, source_hbm, kind_hbm,
    hid_ref, gs_ref, gn_ref,
    x_own, wanted_ref, pats, cot, count_ref, source_ref, kind_ref,
    ext, halo_out, mean, xm, weights, partial, grad, other, other_in,
    part_a, part_a_in, part_b, part_b_in, kept_a, kept_b,
    col_a, col_a_in, col_b, col_b_in, fin, cell, cell_in, final,
    sem_out, sem_in, load_sem,
):
    nx, nz = FEAT_GRID
    ny, nc = DOM_GRID
    nf, nd, hz = nx * nz, ny * nc, nz // 2
    feat = lax.axis_index("feat")
    dom = lax.axis_index("dom")
    x, z = feat // nz, feat % nz
    y, core = dom // nc, dom % nc
    half, zz = z // hz, z % hz
    slot = half * (nx * hz) + x * hz + zz
    width = x_own.shape[0]
    depth = nx * hz * width
    band = hz * width
    tiles = nf
    slot_tiles = halo_out.shape[1]
    slots = wanted_ref.shape[1]
    steps = source_ref.shape[0]

    def send(src, dst, phase, where):
        pltpu.make_async_remote_copy(
            src_ref=src, dst_ref=dst, send_sem=sem_out.at[phase], recv_sem=sem_in.at[phase],
            device_id=where, device_id_type=MESH,
        ).start()

    def feat_at(fx, fz):
        return {"feat": fx * nz + fz, "dom": dom}

    def dom_at(dy, dc):
        return {"feat": feat, "dom": dy * nc + dc}

    block = pl.ds(pl.multiple_of(y * 128, 128), 128)
    my_unit = weights.at[half, core, y, x, zz]
    loads = [
        pltpu.make_async_copy(src, dst, load_sem.at[i])
        for i, (src, dst) in enumerate((
            (x_hbm, x_own), (rows_hbm.at[dom], wanted_ref), (count_hbm, count_ref),
            (pat_hbm, pats), (source_hbm, source_ref), (kind_hbm, kind_ref), (cot_hbm, cot),
        ))
    ]
    for load in loads:
        load.start()

    @pl.when(core == 0)
    def _():
        pltpu.make_async_copy(w1_hbm.at[:, block], my_unit, load_sem.at[7]).start()

    @pl.when(core == 1)
    def _():
        pltpu.make_async_copy(w2_hbm.at[:, block], my_unit, load_sem.at[7]).start()

    barrier = pltpu.get_barrier_semaphore()

    def greet_feat(i, _):
        pl.semaphore_signal(
            barrier, inc=1, device_id={"feat": (feat + i) % nf, "dom": dom}, device_id_type=MESH
        )
        return 0

    def greet_dom(i, _):
        pl.semaphore_signal(
            barrier, inc=1, device_id={"feat": feat, "dom": (dom + i) % nd}, device_id_type=MESH
        )
        return 0

    lax.fori_loop(1, nf, greet_feat, 0)
    lax.fori_loop(1, nd, greet_dom, 0)
    for load in loads[:3]:
        load.wait()

    def take(t, _):
        ext[t] = x_own[:, pl.ds(pl.multiple_of(t * 128, 128), 128)]
        return 0

    lax.fori_loop(0, tiles, take, 0)
    xm[0, slot] = ext[feat]

    group = min(tiles, 16)
    lane_ids = lax.broadcasted_iota(jnp.int32, (128, slots), 0)
    slot_ids = lax.broadcasted_iota(jnp.int32, (1, slots), 1)

    def pick(dest, _):
        wanted = wanted_ref[pl.ds(dest, 1), :]
        low, high = wanted & 127, wanted >> 7
        choose = jnp.where(lane_ids == low, 1.0, 0.0).astype(BF)
        found = jnp.zeros((width, slots), F32)
        for g in range(0, tiles, group):
            rows = ext[g : g + group].reshape(group * width, 128)
            spread = jnp.dot(rows, choose, preferred_element_type=F32)
            for h in range(group):
                found = jnp.where(
                    high == g + h, spread[h * width : (h + 1) * width], found
                )
        live = slot_ids < count_ref[dom, dest]
        found = jnp.where(live, found, 0.0).astype(BF)
        for j in range(slot_tiles):
            halo_out[dest, j] = found[:, j * 128 : (j + 1) * 128]
        return 0

    lax.fori_loop(0, nd, pick, 0)
    halo_at = tiles + dom * slot_tiles
    for j in range(slot_tiles):
        ext[halo_at + j] = halo_out[dom, j]
    pltpu.make_async_copy(my_unit, my_unit, load_sem.at[7]).wait()
    for load in loads[3:]:
        load.wait()
    pl.semaphore_wait(barrier, nf - 1 + nd - 1)

    def halo_send(i, _):
        dest = (dom + i) % nd
        send(
            halo_out.at[dest], ext.at[pl.ds(halo_at, slot_tiles)], 0,
            {"feat": feat, "dom": dest},
        )
        return 0

    lax.fori_loop(1, nd, halo_send, 0)

    def weights_z(i, _):
        send(my_unit, my_unit, 1, feat_at(x, (z + i) % nz))
        return 0

    lax.fori_loop(1, nz, weights_z, 0)

    def features_out(i, _):
        peer = (feat + i) % nf
        send(ext.at[peer], xm.at[0, slot], 2, {"feat": peer, "dom": dom})
        return 0

    lax.fori_loop(1, nf, features_out, 0)

    ones = jnp.ones((width, 256), BF)

    def mean_of(t):
        total = jnp.zeros((2 * width, 128), F32)
        for k in range(0, steps, 2):
            left = jnp.concatenate([ext[source_ref[k, t]], ext[source_ref[k + 1, t]]], axis=1)
            right = jnp.concatenate([pats[kind_ref[k, t]], pats[kind_ref[k + 1, t]]], axis=1)
            total = total + lax.dot_general(
                jnp.concatenate([left, ones], axis=0), right, (((1,), (1,)), ((), ())),
                preferred_element_type=F32,
            )
        return (total[:width] / total[width : width + 1]).astype(BF)

    def mean_out(i, _):
        peers = [(feat + 1 + 2 * i + j) % nf for j in range(2)]
        found = [mean_of(peer) for peer in peers]
        for peer, value in zip(peers, found):
            mean[peer] = value
        for peer in peers:

            @pl.when(peer != feat)
            def _():
                send(mean.at[peer], xm.at[1, slot], 3, {"feat": peer, "dom": dom})

        return 0

    drain(ext.at[pl.ds(tiles, (nd - 1) * slot_tiles)], sem_in.at[0])
    lax.fori_loop(0, nf // 2, mean_out, 0)
    xm[1, slot] = mean[feat]

    drain(ext.at[pl.ds(0, nz - 1)], sem_in.at[1])
    first_a, first_b = weights.at[0, core, y, x], weights.at[1, core, y, x]
    for i in range(1, nx):
        send(first_a, first_a, 4, feat_at((x + i) % nx, z))
    for i in range(1, ny):
        send(first_b, first_b, 5, dom_at((y + i) % ny, core))
    drain(weights.at[0, core, y, pl.ds(0, nx - 1)], sem_in.at[4])
    then_a = weights.at[0, core, y]
    for i in range(1, ny):
        send(then_a, then_a, 6, dom_at((y + i) % ny, core))
    drain(weights.at[1, core, pl.ds(0, ny - 1), x], sem_in.at[5])
    then_b = weights.at[1, core, :, x]
    for i in range(1, nx):
        send(then_b, then_b, 7, feat_at((x + i) % nx, z))
    drain(weights.at[0, core, pl.ds(0, ny - 1)], sem_in.at[6])
    drain(weights.at[1, core, :, pl.ds(0, nx - 1)], sem_in.at[7])
    for h in range(2):
        send(weights.at[h, core], weights.at[h, core], 8, dom_at(y, 1 - core))
    drain(xm.at[0, pl.ds(0, nf - 1)], sem_in.at[2])

    def times_weights(m, own, b):
        total = jnp.zeros((128, 128), F32)
        for h in range(2):
            total = total + lax.dot_general(
                own[h], weights[h, m, b].reshape(depth, 128), (((0,), (0,)), ((), ())),
                preferred_element_type=F32,
            )
        return total

    def halves(m):
        return [xm[m, h * nx * hz : (h + 1) * nx * hz].reshape(depth, 128) for h in range(2)]

    drain(weights.at[0], sem_in.at[8])
    own = halves(0)
    for b in range(ny):
        partial[:, b * 128 : (b + 1) * 128] = times_weights(0, own, b)
    drain(xm.at[1, pl.ds(0, nf - 1)], sem_in.at[3])
    own = halves(1)
    for b in range(ny):
        span = slice(b * 128, (b + 1) * 128)
        value, slope = gelu_pair(partial[:, span] + times_weights(1, own, b))
        hid_ref[:, span] = value.astype(BF)
        grad[:, span] = (cot[:, span].astype(F32) * slope).astype(BF)

    def product(m, h, b):
        rows = xm[m, pl.ds(h * nx * hz + b * hz, hz)].reshape(band, 128)
        return jnp.dot(rows, grad[...], preferred_element_type=F32)

    for h in range(2):

        def core_out(b, _, h=h):
            result = product(1 - core, h, b).astype(BF)
            for c in range(ny):
                other[h, b, c] = result[:, c * 128 : (c + 1) * 128]
            return 0

        lax.fori_loop(0, nx, core_out, 0)
        send(other.at[h], other_in.at[h], 9 + h, dom_at(y, 1 - core))

    drain(other_in.at[0], sem_in.at[9])

    def y_first(b, _):
        result = product(core, 0, b)
        for c in range(ny):
            summed = result[:, c * 128 : (c + 1) * 128] + other_in[0, b, c].astype(F32)
            part_a[c, b] = summed.astype(BF)

            @pl.when(c == y)
            def _():
                kept_a[b] = summed

        return 0

    lax.fori_loop(0, nx, y_first, 0)
    for i in range(1, ny):
        c = (y + i) % ny
        send(part_a.at[c], part_a_in.at[y], 11, dom_at(c, core))

    drain(other_in.at[1], sem_in.at[10])

    def x_first(b, _):
        result = product(core, 1, b)
        for c in range(ny):
            summed = result[:, c * 128 : (c + 1) * 128] + other_in[1, b, c].astype(F32)
            part_b[b, c] = summed.astype(BF)

            @pl.when(b == x)
            def _():
                kept_b[c] = summed

        return 0

    lax.fori_loop(0, nx, x_first, 0)
    for i in range(1, nx):
        b = (x + i) % nx
        send(part_b.at[b], part_b_in.at[x], 12, feat_at(b, z))

    def y_sum(b):
        total = kept_a[b]
        for j in range(1, ny):
            total = total + part_a_in[(y + j) % ny, b].astype(F32)
        return total

    def x_sum(c):
        total = kept_b[c]
        for j in range(1, nx):
            total = total + part_b_in[(x + j) % nx, c].astype(F32)
        return total

    drain(part_a_in.at[pl.ds(0, ny - 1)], sem_in.at[11])

    def x_then(i, _):
        b = (x + i) % nx
        col_a[b] = y_sum(b).astype(BF)
        send(col_a.at[b], col_a_in.at[x], 13, feat_at(b, z))
        return 0

    lax.fori_loop(1, nx, x_then, 0)
    fin[0] = y_sum(x)

    drain(part_b_in.at[pl.ds(0, nx - 1)], sem_in.at[12])

    def y_then(i, _):
        c = (y + i) % ny
        col_b[c] = x_sum(c).astype(BF)
        send(col_b.at[c], col_b_in.at[y], 14, dom_at(c, core))
        return 0

    lax.fori_loop(1, ny, y_then, 0)
    fin[1] = x_sum(y)

    def z_out(i, _):
        peer = i

        @pl.when(peer != z)
        def _():
            send(cell.at[peer], cell_in.at[z], 15, feat_at(x, peer))

        return 0

    drain(col_a_in.at[pl.ds(0, nx - 1)], sem_in.at[13])
    total = fin[0]
    for j in range(1, nx):
        total = total + col_a_in[(x + j) % nx].astype(F32)
    fin[0] = total
    cell[0:hz] = total.astype(BF).reshape(hz, width, 128)
    lax.fori_loop(0, hz, z_out, 0)
    drain(col_b_in.at[pl.ds(0, ny - 1)], sem_in.at[14])
    total = fin[1]
    for j in range(1, ny):
        total = total + col_b_in[(y + j) % ny].astype(F32)
    fin[1] = total
    cell[hz:nz] = total.astype(BF).reshape(hz, width, 128)
    lax.fori_loop(hz, nz, z_out, 0)
    drain(cell_in.at[pl.ds(0, nz - 1)], sem_in.at[15])
    total = fin[half, pl.ds(pl.multiple_of(zz * width, width), width)]
    for j in range(1, nz):
        total = total + cell_in[(z + j) % nz].astype(F32)

    final[dom] = total

    def dom_out(i, _):
        send(final.at[dom], final.at[dom], 16, {"feat": feat, "dom": (dom + i) % nd})
        return 0

    lax.fori_loop(1, nd, dom_out, 0)
    drain(final.at[pl.ds(0, nd - 1)], sem_in.at[16])
    for b in range(ny):
        span = slice(b * 128, (b + 1) * 128)
        gs_ref[:, span] = final[b * nc]
        gn_ref[:, span] = final[b * nc + 1]

    sent = (
        halo_out.at[pl.ds(0, nd - 1)], ext.at[pl.ds(0, nz - 1)], ext.at[pl.ds(0, nf - 1)],
        mean.at[pl.ds(0, nf - 1)], weights.at[0, core, y, pl.ds(0, nx - 1)],
        weights.at[1, core, pl.ds(0, ny - 1), x], weights.at[0, core, pl.ds(0, ny - 1)],
        weights.at[1, core, :, pl.ds(0, nx - 1)], weights.at[0], other.at[0], other.at[1],
        part_a.at[pl.ds(0, ny - 1)], part_b.at[pl.ds(0, nx - 1)],
        col_a.at[pl.ds(0, nx - 1)], col_b.at[pl.ds(0, ny - 1)], cell.at[pl.ds(0, nz - 1)],
        final.at[pl.ds(0, nd - 1)],
    )
    for phase, ref in enumerate(sent):
        drain(ref, sem_out.at[phase])


def store_out(hid_in, gs_in, gn_in, hid_ref, gs_ref, gn_ref, sems):
    pairs = ((hid_in, hid_ref), (gs_in, gs_ref), (gn_in, gn_ref))
    copies = [pltpu.make_async_copy(a, b, sems.at[i]) for i, (a, b) in enumerate(pairs)]
    for copy in copies:
        copy.start()
    for copy in copies:
        copy.wait()


def on_device(features, w1, w2, cotangent, send_rows, send_count, tile_source, tile_kind, patterns):
    nx, nz = FEAT_GRID
    ny, nc = DOM_GRID
    nf, nd, hz = nx * nz, ny * nc, nz // 2
    width = features.shape[1]
    hidden = w1.shape[1]
    slot_tiles = send_rows.shape[2] // 128
    assert features.shape[0] == nf * 128 and hidden == ny * 128 and nc == 2
    band = hz * width
    vmem = pl.BlockSpec(memory_space=pltpu.VMEM)
    hbm = pl.BlockSpec(memory_space=pltpu.HBM)
    source, kind = tile_source[0].T, tile_kind[0].T
    shapes = (
        jax.ShapeDtypeStruct((128, hidden), BF),
        jax.ShapeDtypeStruct((width, hidden), F32),
        jax.ShapeDtypeStruct((width, hidden), F32),
    )
    results = pl.pallas_call(
        layer,
        out_shape=shapes,
        in_specs=[hbm] * 9,
        out_specs=(vmem,) * 3,
        scratch_shapes=[
            pltpu.VMEM((width, nf * 128), BF),
            pltpu.VMEM(send_rows.shape[1:], jnp.int32),
            pltpu.VMEM(patterns.shape, BF),
            pltpu.VMEM((128, hidden), BF),
            pltpu.SMEM(send_count.shape, jnp.int32),
            pltpu.SMEM(source.shape, jnp.int32),
            pltpu.SMEM(kind.shape, jnp.int32),
            pltpu.VMEM((nf + nd * slot_tiles, width, 128), BF),
            pltpu.VMEM((nd, slot_tiles, width, 128), BF),
            pltpu.VMEM((nf, width, 128), BF),
            pltpu.VMEM((2, nf, width, 128), BF),
            pltpu.VMEM((2, nc, ny, nx, hz, width, 128), BF),
            pltpu.VMEM((128, hidden), F32),
            pltpu.VMEM((128, hidden), BF),
            pltpu.VMEM((2, nx, ny, band, 128), BF),
            pltpu.VMEM((2, nx, ny, band, 128), BF),
            pltpu.VMEM((ny, nx, band, 128), BF),
            pltpu.VMEM((ny, nx, band, 128), BF),
            pltpu.VMEM((nx, ny, band, 128), BF),
            pltpu.VMEM((nx, ny, band, 128), BF),
            pltpu.VMEM((nx, band, 128), F32),
            pltpu.VMEM((ny, band, 128), F32),
            pltpu.VMEM((nx, band, 128), BF),
            pltpu.VMEM((nx, band, 128), BF),
            pltpu.VMEM((ny, band, 128), BF),
            pltpu.VMEM((ny, band, 128), BF),
            pltpu.VMEM((2, band, 128), F32),
            pltpu.VMEM((nz, width, 128), BF),
            pltpu.VMEM((nz, width, 128), BF),
            pltpu.VMEM((nd, width, 128), F32),
            pltpu.SemaphoreType.DMA((17,)),
            pltpu.SemaphoreType.DMA((17,)),
            pltpu.SemaphoreType.DMA((8,)),
        ],
        compiler_params=pltpu.CompilerParams(
            collective_id=0, has_side_effects=True, vmem_limit_bytes=48 << 20
        ),
    )(
        features.T, w1, w2, cotangent, send_rows, patterns, send_count, source, kind,
    )
    anywhere = pl.BlockSpec(memory_space=pl.ANY)
    return pl.pallas_call(
        store_out,
        out_shape=shapes,
        in_specs=[anywhere] * 3,
        out_specs=(hbm,) * 3,
        scratch_shapes=[pltpu.SemaphoreType.DMA((3,))],
    )(*results)


def solution(mesh):
    placed = (
        P("dom", "feat"),
        P("feat", None),
        P("feat", None),
        P(("dom", "feat"), None),
        P(),
        P(),
        P("dom", None, None),
        P("dom", None, None),
        P(),
    )
    return jax.shard_map(
        on_device,
        mesh=mesh,
        in_specs=placed,
        out_specs=(P(("dom", "feat"), None), P("feat", None), P("feat", None)),
        check_vma=False,
    )
```

time: 92 us -> 94.6 us (1.028)
  Pallas kernels: 81.3 us -> 83.8 us
    pallas_call x1 -> x2, Pallas kernels: 81.3 us -> 83.8 us  [the longest x1 76.7 us: on_device(): pl.pallas_call(layer, out_shape=shapes, in_specs=[hbm] * 9, out_specs=(vm...]
    unnamed x21 -> x24, local copies, waits for them, and re-layouts: 9.66 us -> 9.62 us
where the time goes in v2:
time: 94.6 us; the launch traced here: 94.1 us
  Pallas kernels  83.8 us (89%)
  local copies, waits for them, and re-layouts  9.62 us (10%)
    pallas_call x1, Pallas kernels, on_device(): pl.pallas_call(layer, out_shape=shapes, in_specs=[hbm] * 9, out_specs=(vm...  76.7 us
    unnamed x24, local copies, waits for them, and re-layouts  9.62 us
    pallas_call x1, Pallas kernels, on_device(): pl.pallas_call(store_out, out_shape=shapes, in_specs=[anywhere] * 3, out_...  7.08 us

profile of v2, /device:TPU:1, one launch (start us, length us, event | category | flops | bytes accessed | tf_op | source)
XLA Modules:
  0.0 94.1 jit_solution(10067917961848261123)
XLA Ops:
  0.6 0.0 copy-start
  0.6 1.6 %copy-done = bf16[64,128,128]{2,1,0:T(8,128)(2,1)S(1)} copy-done((bf16[64,128,128]{2,1,0:T(8,128)(2,1)S(1)}, bf16[64,128,128]{2,1,0:T(8,128)(2,1)}, u32[]{:S(2)}) %copy-start) | copy-done | bytes 2097176
  2.2 0.0 copy-start.1
  2.2 0.9 %copy-done.1 = bf16[8192,16]{0,1:T(8,128)(2,1)S(1)} copy-done((bf16[8192,16]{0,1:T(8,128)(2,1)S(1)}, bf16[8192,16]{0,1:T(8,128)(2,1)}, u32[]{:S(2)}) %copy-start.1) | copy-done | bytes 262168
  3.2 0.0 copy-start.2
  3.2 0.9 copy-done.2
  4.1 0.0 copy-start.4
  4.1 0.8 copy-done.4
  4.9 0.0 copy-start.7
  4.9 0.7 copy-done.7
  5.6 0.0 copy-start.8
  5.6 0.7 copy-done.8
  6.4 0.0 copy-start.9
  6.4 0.7 copy-done.9
  7.0 0.0 copy-start.10
  7.0 0.7 copy-done.10
  7.7 0.0 copy-start.11
  7.7 0.7 copy-done.11
  8.4 76.7 %shard_map.112 = (bf16[128,512]{1,0:T(8,128)(2,1)S(1)}, f32[16,512]{1,0:T(8,128)S(1)}, f32[16,512]{1,0:T(8,128)S(1)}) custom-call(bf16[16,8192]{1,0:T(8,128)(2,1)S(1)} %bitcast.7, bf16[16,512]{1,0:T(8,128)(2,1)S(1)} %copy-done.7, bf16[16,512]{1,0:T(8,128)(2,1)S(1)} %copy-done.8, bf16[128,512]{1,0:T(8,128)(2,1)S(1)} %copy-done.2, s32[8,8,256]{2,1,0:T(8,128)S(1)} %copy-done.4, ...), custom_call_target="tpu_custom_call" | custom-call | tf_op jit(solution)/shard_map/pallas_call | solution.py:406
  85.2 0.0 copy-start.3
  85.2 0.6 copy-done.3
  85.8 0.0 copy-start.5
  85.8 0.6 copy-done.5
  86.4 0.0 copy-start.6
  86.4 0.6 copy-done.6
  87.0 7.1 %shard_map.113 = (bf16[128,512]{1,0:T(8,128)(2,1)}, f32[16,512]{1,0:T(8,128)}, f32[16,512]{1,0:T(8,128)}) custom-call(bf16[128,512]{1,0:T(8,128)(2,1)} %copy-done.3, f32[16,512]{1,0:T(8,128)} %copy-done.5, f32[16,512]{1,0:T(8,128)} %copy-done.6), custom_call_target="tpu_custom_call" | custom-call | tf_op jit(solution)/shard_map/pallas_call | solution.py:453
Async XLA Ops:
  0.6 1.6 %copy-start = (bf16[64,128,128]{2,1,0:T(8,128)(2,1)S(1)}, bf16[64,128,128]{2,1,0:T(8,128)(2,1)}, u32[]{:S(2)}) copy-start(bf16[64,128,128]{2,1,0:T(8,128)(2,1)} %pat_hbm.1) | copy-start | bytes 6291460
  2.2 0.9 %copy-start.1 = (bf16[8192,16]{0,1:T(8,128)(2,1)S(1)}, bf16[8192,16]{0,1:T(8,128)(2,1)}, u32[]{:S(2)}) copy-start(bf16[8192,16]{0,1:T(8,128)(2,1)} %param.9) | copy-start | bytes 786436
  3.2 0.9 copy-start.2
  4.1 0.8 copy-start.4
  4.9 0.7 copy-start.7
  5.6 0.7 copy-start.8
  6.4 0.7 copy-start.9
  7.0 0.7 copy-start.10
  7.7 0.7 copy-start.11
  85.2 0.7 copy-start.3
  85.8 0.6 copy-start.5
  86.4 0.6 copy-start.6

commit v3 on v2

--- a/solution.py
+++ b/solution.py
@@ -377,15 +377,6 @@
         drain(ref, sem_out.at[phase])
 
 
-def store_out(hid_in, gs_in, gn_in, hid_ref, gs_ref, gn_ref, sems):
-    pairs = ((hid_in, hid_ref), (gs_in, gs_ref), (gn_in, gn_ref))
-    copies = [pltpu.make_async_copy(a, b, sems.at[i]) for i, (a, b) in enumerate(pairs)]
-    for copy in copies:
-        copy.start()
-    for copy in copies:
-        copy.wait()
-
-
 def on_device(features, w1, w2, cotangent, send_rows, send_count, tile_source, tile_kind, patterns):
     nx, nz = FEAT_GRID
     ny, nc = DOM_GRID
@@ -403,7 +394,7 @@
         jax.ShapeDtypeStruct((width, hidden), F32),
         jax.ShapeDtypeStruct((width, hidden), F32),
     )
-    results = pl.pallas_call(
+    return pl.pallas_call(
         layer,
         out_shape=shapes,
         in_specs=[hbm] * 9,
@@ -444,19 +435,11 @@
             pltpu.SemaphoreType.DMA((8,)),
         ],
         compiler_params=pltpu.CompilerParams(
-            collective_id=0, has_side_effects=True, vmem_limit_bytes=48 << 20
+            collective_id=0, has_side_effects=True, vmem_limit_bytes=67_000_000
         ),
     )(
         features.T, w1, w2, cotangent, send_rows, patterns, send_count, source, kind,
     )
-    anywhere = pl.BlockSpec(memory_space=pl.ANY)
-    return pl.pallas_call(
-        store_out,
-        out_shape=shapes,
-        in_specs=[anywhere] * 3,
-        out_specs=(hbm,) * 3,
-        scratch_shapes=[pltpu.SemaphoreType.DMA((3,))],
-    )(*results)
 
 
 def solution(mesh):

time: 94.6 us -> 82.3 us (0.87)
  Pallas kernels: 83.8 us -> 77.1 us
  local copies, waits for them, and re-layouts: 9.62 us -> 4.32 us
    pallas_call x1 -> x0, Pallas kernels: 7.08 us -> none  [on_device(): pl.pallas_call(store_out, out_shape=shapes, in_specs=[anywhere] * 3, out_...]
    unnamed x24 -> x3, local copies, waits for them, and re-layouts: 9.62 us -> 4.32 us
where the time goes in v3:
time: 82.3 us; the launch traced here: 82.1 us
  Pallas kernels  77.1 us (94%)
  local copies, waits for them, and re-layouts  4.32 us (5%)
    pallas_call x1, Pallas kernels, on_device(): pl.pallas_call(layer, out_shape=shapes, in_specs=[hbm] * 9, out_specs=(vm...  77.1 us
    unnamed x3, local copies, waits for them, and re-layouts  4.32 us

profile of v3, /device:TPU:1, one launch (start us, length us, event | category | flops | bytes accessed | tf_op | source)
XLA Modules:
  0.0 82.1 jit_solution(18144252646434560310)
XLA Ops:
  0.6 77.1 %shard_map.112 = (bf16[128,512]{1,0:T(8,128)(2,1)}, f32[16,512]{1,0:T(8,128)}, f32[16,512]{1,0:T(8,128)}) custom-call(bf16[16,8192]{1,0:T(8,128)(2,1)} %bitcast.7, bf16[16,512]{1,0:T(8,128)(2,1)} %w1_hbm.1, bf16[16,512]{1,0:T(8,128)(2,1)} %w2_hbm.1, bf16[128,512]{1,0:T(8,128)(2,1)} %cot_hbm.1, s32[8,8,256]{2,1,0:T(8,128)} %rows_hbm.1, ...), custom_call_target="tpu_custom_call" | custom-call | tf_op jit(solution)/shard_map/pallas_call | solution.py:397
  77.7 1.6 %copy.15 = bf16[128,512]{1,0:T(8,128)(2,1)} copy(bf16[128,512]{1,0:T(8,128)(2,1)} %get-tuple-element.6) | data formatting | bytes 262144
  79.3 1.4 %copy.16 = f32[16,512]{1,0:T(8,128)} copy(f32[16,512]{1,0:T(8,128)} %get-tuple-element.7) | data formatting | bytes 65536
  80.7 1.4 %copy.17 = f32[16,512]{1,0:T(8,128)} copy(f32[16,512]{1,0:T(8,128)} %get-tuple-element.8) | data formatting | bytes 65536

commit v4 on v3

--- a/solution.py
+++ b/solution.py
@@ -28,7 +28,7 @@
     x_hbm, w1_hbm, w2_hbm, cot_hbm, rows_hbm, pat_hbm, count_hbm, source_hbm, kind_hbm,
     hid_ref, gs_ref, gn_ref,
     x_own, wanted_ref, pats, cot, count_ref, source_ref, kind_ref,
-    ext, halo_out, mean, xm, weights, partial, grad, other, other_in,
+    ext, halo_out, mean, xm, weights, partial, grad, other_a, other_a_in, other_b, other_b_in,
     part_a, part_a_in, part_b, part_b_in, kept_a, kept_b,
     col_a, col_a_in, col_b, col_b_in, fin, cell, cell_in, final,
     sem_out, sem_in, load_sem,
@@ -71,22 +71,11 @@
             (pat_hbm, pats), (source_hbm, source_ref), (kind_hbm, kind_ref), (cot_hbm, cot),
         ))
     ]
-    for load in loads:
-        load.start()
-
-    @pl.when(core == 0)
-    def _():
-        pltpu.make_async_copy(w1_hbm.at[:, block], my_unit, load_sem.at[7]).start()
-
-    @pl.when(core == 1)
-    def _():
-        pltpu.make_async_copy(w2_hbm.at[:, block], my_unit, load_sem.at[7]).start()
-
     barrier = pltpu.get_barrier_semaphore()
 
     def greet_feat(i, _):
         pl.semaphore_signal(
-            barrier, inc=1, device_id={"feat": (feat + i) % nf, "dom": dom}, device_id_type=MESH
+            barrier, inc=1, device_id={"feat": (feat + far + i) % nf, "dom": dom}, device_id_type=MESH
         )
         return 0
 
@@ -96,8 +85,21 @@
         )
         return 0
 
-    lax.fori_loop(1, nf, greet_feat, 0)
+    far = hz
+    lax.fori_loop(0, nf - hz, greet_feat, 0)
+    lax.fori_loop(nf - hz + 1, nf, greet_feat, 0)
     lax.fori_loop(1, nd, greet_dom, 0)
+    for load in loads:
+        load.start()
+
+    @pl.when(core == 0)
+    def _():
+        pltpu.make_async_copy(w1_hbm.at[:, block], my_unit, load_sem.at[7]).start()
+
+    @pl.when(core == 1)
+    def _():
+        pltpu.make_async_copy(w2_hbm.at[:, block], my_unit, load_sem.at[7]).start()
+
     for load in loads[:3]:
         load.wait()
 
@@ -236,58 +238,77 @@
         hid_ref[:, span] = value.astype(BF)
         grad[:, span] = (cot[:, span].astype(F32) * slope).astype(BF)
 
-    def product(m, h, b):
-        rows = xm[m, pl.ds(h * nx * hz + b * hz, hz)].reshape(band, 128)
-        return jnp.dot(rows, grad[...], preferred_element_type=F32)
-
-    for h in range(2):
-
-        def core_out(b, _, h=h):
-            result = product(1 - core, h, b).astype(BF)
+    def rows_of(m, h, b):
+        return xm[m, pl.ds(h * nx * hz + b * hz, hz)].reshape(band, 128)
+
+    def product_a(m, b):
+        return jnp.dot(rows_of(m, 0, b), grad[...], preferred_element_type=F32)
+
+    def product_b(m, b, p):
+        columns = grad[:, p * cb * 128 : (p + 1) * cb * 128]
+        return jnp.dot(rows_of(m, 1, b), columns, preferred_element_type=F32)
+
+    ca, cb = nx // 2, ny // 2
+    for p in range(2):
+
+        def core_a(b, _):
+            result = product_a(1 - core, b).astype(BF)
             for c in range(ny):
-                other[h, b, c] = result[:, c * 128 : (c + 1) * 128]
+                other_a[b, c] = result[:, c * 128 : (c + 1) * 128]
             return 0
 
-        lax.fori_loop(0, nx, core_out, 0)
-        send(other.at[h], other_in.at[h], 9 + h, dom_at(y, 1 - core))
-
-    drain(other_in.at[0], sem_in.at[9])
-
-    def y_first(b, _):
-        result = product(core, 0, b)
-        for c in range(ny):
-            summed = result[:, c * 128 : (c + 1) * 128] + other_in[0, b, c].astype(F32)
-            part_a[c, b] = summed.astype(BF)
-
-            @pl.when(c == y)
-            def _():
-                kept_a[b] = summed
-
-        return 0
-
-    lax.fori_loop(0, nx, y_first, 0)
-    for i in range(1, ny):
-        c = (y + i) % ny
-        send(part_a.at[c], part_a_in.at[y], 11, dom_at(c, core))
-
-    drain(other_in.at[1], sem_in.at[10])
-
-    def x_first(b, _):
-        result = product(core, 1, b)
-        for c in range(ny):
-            summed = result[:, c * 128 : (c + 1) * 128] + other_in[1, b, c].astype(F32)
-            part_b[b, c] = summed.astype(BF)
-
-            @pl.when(b == x)
-            def _():
-                kept_b[c] = summed
-
-        return 0
-
-    lax.fori_loop(0, nx, x_first, 0)
-    for i in range(1, nx):
-        b = (x + i) % nx
-        send(part_b.at[b], part_b_in.at[x], 12, feat_at(b, z))
+        def core_b(b, _, p=p):
+            result = product_b(1 - core, b, p).astype(BF)
+            for c in range(cb):
+                other_b[p * cb + c, b] = result[:, c * 128 : (c + 1) * 128]
+            return 0
+
+        lax.fori_loop(p * ca, (p + 1) * ca, core_a, 0)
+        piece = pl.ds(p * ca, ca)
+        send(other_a.at[piece], other_a_in.at[piece], 9 + p, dom_at(y, 1 - core))
+        lax.fori_loop(0, nx, core_b, 0)
+        piece = pl.ds(p * cb, cb)
+        send(other_b.at[piece], other_b_in.at[piece], 11 + p, dom_at(y, 1 - core))
+
+    for p in range(2):
+
+        def y_first(b, _):
+            result = product_a(core, b)
+            for c in range(ny):
+                summed = result[:, c * 128 : (c + 1) * 128] + other_a_in[b, c].astype(F32)
+                part_a[c, b] = summed.astype(BF)
+
+                @pl.when(c == y)
+                def _():
+                    kept_a[b] = summed
+
+            return 0
+
+        def x_first(b, _, p=p):
+            result = product_b(core, b, p)
+            for c in range(cb):
+                column = p * cb + c
+                summed = result[:, c * 128 : (c + 1) * 128] + other_b_in[column, b].astype(F32)
+                part_b[b, column] = summed.astype(BF)
+
+                @pl.when(b == x)
+                def _():
+                    kept_b[column] = summed
+
+            return 0
+
+        piece = pl.ds(p * ca, ca)
+        drain(other_a_in.at[piece], sem_in.at[9 + p])
+        lax.fori_loop(p * ca, (p + 1) * ca, y_first, 0)
+        for i in range(1, ny):
+            c = (y + i) % ny
+            send(part_a.at[c, piece], part_a_in.at[y, piece], 13, dom_at(c, core))
+        piece = pl.ds(p * cb, cb)
+        drain(other_b_in.at[piece], sem_in.at[11 + p])
+        lax.fori_loop(0, nx, x_first, 0)
+        for i in range(1, nx):
+            b = (x + i) % nx
+            send(part_b.at[b, piece], part_b_in.at[x, piece], 14, feat_at(b, z))
 
     def y_sum(b):
         total = kept_a[b]
@@ -301,23 +322,23 @@
             total = total + part_b_in[(x + j) % nx, c].astype(F32)
         return total
 
-    drain(part_a_in.at[pl.ds(0, ny - 1)], sem_in.at[11])
+    drain(part_a_in.at[pl.ds(0, ny - 1)], sem_in.at[13])
 
     def x_then(i, _):
         b = (x + i) % nx
         col_a[b] = y_sum(b).astype(BF)
-        send(col_a.at[b], col_a_in.at[x], 13, feat_at(b, z))
+        send(col_a.at[b], col_a_in.at[x], 15, feat_at(b, z))
         return 0
 
     lax.fori_loop(1, nx, x_then, 0)
     fin[0] = y_sum(x)
 
-    drain(part_b_in.at[pl.ds(0, nx - 1)], sem_in.at[12])
+    drain(part_b_in.at[pl.ds(0, nx - 1)], sem_in.at[14])
 
     def y_then(i, _):
         c = (y + i) % ny
         col_b[c] = x_sum(c).astype(BF)
-        send(col_b.at[c], col_b_in.at[y], 14, dom_at(c, core))
+        send(col_b.at[c], col_b_in.at[y], 16, dom_at(c, core))
         return 0
 
     lax.fori_loop(1, ny, y_then, 0)
@@ -328,25 +349,25 @@
 
         @pl.when(peer != z)
         def _():
-            send(cell.at[peer], cell_in.at[z], 15, feat_at(x, peer))
-
-        return 0
-
-    drain(col_a_in.at[pl.ds(0, nx - 1)], sem_in.at[13])
+            send(cell.at[peer], cell_in.at[z], 17, feat_at(x, peer))
+
+        return 0
+
+    drain(col_a_in.at[pl.ds(0, nx - 1)], sem_in.at[15])
     total = fin[0]
     for j in range(1, nx):
         total = total + col_a_in[(x + j) % nx].astype(F32)
     fin[0] = total
     cell[0:hz] = total.astype(BF).reshape(hz, width, 128)
     lax.fori_loop(0, hz, z_out, 0)
-    drain(col_b_in.at[pl.ds(0, ny - 1)], sem_in.at[14])
+    drain(col_b_in.at[pl.ds(0, ny - 1)], sem_in.at[16])
     total = fin[1]
     for j in range(1, ny):
         total = total + col_b_in[(y + j) % ny].astype(F32)
     fin[1] = total
     cell[hz:nz] = total.astype(BF).reshape(hz, width, 128)
     lax.fori_loop(hz, nz, z_out, 0)
-    drain(cell_in.at[pl.ds(0, nz - 1)], sem_in.at[15])
+    drain(cell_in.at[pl.ds(0, nz - 1)], sem_in.at[17])
     total = fin[half, pl.ds(pl.multiple_of(zz * width, width), width)]
     for j in range(1, nz):
         total = total + cell_in[(z + j) % nz].astype(F32)
@@ -354,11 +375,11 @@
     final[dom] = total
 
     def dom_out(i, _):
-        send(final.at[dom], final.at[dom], 16, {"feat": feat, "dom": (dom + i) % nd})
+        send(final.at[dom], final.at[dom], 18, {"feat": feat, "dom": (dom + i) % nd})
         return 0
 
     lax.fori_loop(1, nd, dom_out, 0)
-    drain(final.at[pl.ds(0, nd - 1)], sem_in.at[16])
+    drain(final.at[pl.ds(0, nd - 1)], sem_in.at[18])
     for b in range(ny):
         span = slice(b * 128, (b + 1) * 128)
         gs_ref[:, span] = final[b * nc]
@@ -368,13 +389,34 @@
         halo_out.at[pl.ds(0, nd - 1)], ext.at[pl.ds(0, nz - 1)], ext.at[pl.ds(0, nf - 1)],
         mean.at[pl.ds(0, nf - 1)], weights.at[0, core, y, pl.ds(0, nx - 1)],
         weights.at[1, core, pl.ds(0, ny - 1), x], weights.at[0, core, pl.ds(0, ny - 1)],
-        weights.at[1, core, :, pl.ds(0, nx - 1)], weights.at[0], other.at[0], other.at[1],
+        weights.at[1, core, :, pl.ds(0, nx - 1)], weights.at[0],
+        other_a.at[pl.ds(0, nx // 2)], other_a.at[pl.ds(0, nx // 2)],
+        other_b.at[pl.ds(0, ny // 2)], other_b.at[pl.ds(0, ny // 2)],
         part_a.at[pl.ds(0, ny - 1)], part_b.at[pl.ds(0, nx - 1)],
         col_a.at[pl.ds(0, nx - 1)], col_b.at[pl.ds(0, ny - 1)], cell.at[pl.ds(0, nz - 1)],
         final.at[pl.ds(0, nd - 1)],
     )
     for phase, ref in enumerate(sent):
         drain(ref, sem_out.at[phase])
+
+
+def store_out(hid_in, gs_in, gn_in, hid_ref, gs_ref, gn_ref, hid_buf, gs_buf, gn_buf, sems):
+    bufs = (hid_buf, gs_buf, gn_buf)
+    ins = [
+        pltpu.make_async_copy(a, b, sems.at[i])
+        for i, (a, b) in enumerate(zip((hid_in, gs_in, gn_in), bufs))
+    ]
+    outs = [
+        pltpu.make_async_copy(a, b, sems.at[3 + i])
+        for i, (a, b) in enumerate(zip(bufs, (hid_ref, gs_ref, gn_ref)))
+    ]
+    for copy in ins:
+        copy.start()
+    for i in range(3):
+        ins[i].wait()
+        outs[i].start()
+    for copy in outs:
+        copy.wait()
 
 
 def on_device(features, w1, w2, cotangent, send_rows, send_count, tile_source, tile_kind, patterns):
@@ -394,7 +436,7 @@
         jax.ShapeDtypeStruct((width, hidden), F32),
         jax.ShapeDtypeStruct((width, hidden), F32),
     )
-    return pl.pallas_call(
+    results = pl.pallas_call(
         layer,
         out_shape=shapes,
         in_specs=[hbm] * 9,
@@ -414,8 +456,10 @@
             pltpu.VMEM((2, nc, ny, nx, hz, width, 128), BF),
             pltpu.VMEM((128, hidden), F32),
             pltpu.VMEM((128, hidden), BF),
-            pltpu.VMEM((2, nx, ny, band, 128), BF),
-            pltpu.VMEM((2, nx, ny, band, 128), BF),
+            pltpu.VMEM((nx, ny, band, 128), BF),
+            pltpu.VMEM((nx, ny, band, 128), BF),
+            pltpu.VMEM((ny, nx, band, 128), BF),
+            pltpu.VMEM((ny, nx, band, 128), BF),
             pltpu.VMEM((ny, nx, band, 128), BF),
             pltpu.VMEM((ny, nx, band, 128), BF),
             pltpu.VMEM((nx, ny, band, 128), BF),
@@ -430,8 +474,8 @@
             pltpu.VMEM((nz, width, 128), BF),
             pltpu.VMEM((nz, width, 128), BF),
             pltpu.VMEM((nd, width, 128), F32),
-            pltpu.SemaphoreType.DMA((17,)),
-            pltpu.SemaphoreType.DMA((17,)),
+            pltpu.SemaphoreType.DMA((19,)),
+            pltpu.SemaphoreType.DMA((19,)),
             pltpu.SemaphoreType.DMA((8,)),
         ],
         compiler_params=pltpu.CompilerParams(
@@ -440,6 +484,15 @@
     )(
         features.T, w1, w2, cotangent, send_rows, patterns, send_count, source, kind,
     )
+    return pl.pallas_call(
+        store_out,
+        out_shape=shapes,
+        in_specs=[hbm] * 3,
+        out_specs=(hbm,) * 3,
+        scratch_shapes=[pltpu.VMEM(a.shape, a.dtype) for a in shapes]
+        + [pltpu.SemaphoreType.DMA((6,))],
+        compiler_params=pltpu.CompilerParams(vmem_limit_bytes=67_000_000),
+    )(*results)
 
 
 def solution(mesh):

time: 82.3 us -> 79.5 us (0.966)
  local copies, waits for them, and re-layouts: 4.32 us -> 0 us
  Pallas kernels: 77.1 us -> 78.7 us
    unnamed x3 -> x0, local copies, waits for them, and re-layouts: 4.32 us -> none
    pallas_call x0 -> x1, Pallas kernels: none -> 1.63 us  [on_device(): pl.pallas_call(store_out, out_shape=shapes, in_specs=[hbm] * 3, out_specs...]
where the time goes in v4:
time: 79.5 us; the launch traced here: 79.4 us
  Pallas kernels  78.7 us (99%)
    pallas_call x1, Pallas kernels, on_device(): pl.pallas_call(layer, out_shape=shapes, in_specs=[hbm] * 9, out_specs=(vm...  77.1 us
    pallas_call x1, Pallas kernels, on_device(): pl.pallas_call(store_out, out_shape=shapes, in_specs=[hbm] * 3, out_specs...  1.63 us

profile of v4, /device:TPU:1, one launch (start us, length us, event | category | flops | bytes accessed | tf_op | source)
XLA Modules:
  0.0 79.4 jit_solution(9723985440905645)
XLA Ops:
  0.6 77.1 %shard_map.112 = (bf16[128,512]{1,0:T(8,128)(2,1)}, f32[16,512]{1,0:T(8,128)}, f32[16,512]{1,0:T(8,128)}) custom-call(bf16[16,8192]{1,0:T(8,128)(2,1)} %bitcast.7, bf16[16,512]{1,0:T(8,128)(2,1)} %w1_hbm.1, bf16[16,512]{1,0:T(8,128)(2,1)} %w2_hbm.1, bf16[128,512]{1,0:T(8,128)(2,1)} %cot_hbm.1, s32[8,8,256]{2,1,0:T(8,128)} %rows_hbm.1, ...), custom_call_target="tpu_custom_call" | custom-call | tf_op jit(solution)/shard_map/pallas_call | solution.py:439
  77.7 1.6 %shard_map.113 = (bf16[128,512]{1,0:T(8,128)(2,1)}, f32[16,512]{1,0:T(8,128)}, f32[16,512]{1,0:T(8,128)}) custom-call(bf16[128,512]{1,0:T(8,128)(2,1)} %get-tuple-element.6.hid_in, f32[16,512]{1,0:T(8,128)} %get-tuple-element.7.gs_in, f32[16,512]{1,0:T(8,128)} %get-tuple-element.8.gn_in), custom_call_target="tpu_custom_call" | custom-call | tf_op jit(solution)/shard_map/pallas_call | solution.py:487

commit v5 on v4

--- a/solution.py
+++ b/solution.py
@@ -31,7 +31,7 @@
     ext, halo_out, mean, xm, weights, partial, grad, other_a, other_a_in, other_b, other_b_in,
     part_a, part_a_in, part_b, part_b_in, kept_a, kept_b,
     col_a, col_a_in, col_b, col_b_in, fin, cell, cell_in, final,
-    sem_out, sem_in, load_sem,
+    sem_out, sem_in, load_sem, round_sem,
 ):
     nx, nz = FEAT_GRID
     ny, nc = DOM_GRID
@@ -73,22 +73,25 @@
     ]
     barrier = pltpu.get_barrier_semaphore()
 
-    def greet_feat(i, _):
-        pl.semaphore_signal(
-            barrier, inc=1, device_id={"feat": (feat + far + i) % nf, "dom": dom}, device_id_type=MESH
-        )
-        return 0
-
-    def greet_dom(i, _):
+    def along(*distances):
+        return sorted(({d % nz for d in distances} | {-d % nz for d in distances}) - {0})
+
+    near = along(1, 2)
+    for i in near:
+        pl.semaphore_signal(barrier, inc=1, device_id=feat_at(x, (z + i) % nz), device_id_type=MESH)
+    for i in range(1, nx):
+        pl.semaphore_signal(barrier, inc=1, device_id=feat_at((x + i) % nx, z), device_id_type=MESH)
+    for i in range(1, nd):
         pl.semaphore_signal(
             barrier, inc=1, device_id={"feat": feat, "dom": (dom + i) % nd}, device_id_type=MESH
         )
-        return 0
-
-    far = hz
-    lax.fori_loop(0, nf - hz, greet_feat, 0)
-    lax.fori_loop(nf - hz + 1, nf, greet_feat, 0)
-    lax.fori_loop(1, nd, greet_dom, 0)
+
+    def round_out(r, offsets):
+        for i in offsets:
+            pl.semaphore_signal(
+                round_sem.at[r], inc=1, device_id=feat_at(x, (z + i) % nz), device_id_type=MESH
+            )
+
     for load in loads:
         load.start()
 
@@ -114,7 +117,10 @@
     lane_ids = lax.broadcasted_iota(jnp.int32, (128, slots), 0)
     slot_ids = lax.broadcasted_iota(jnp.int32, (1, slots), 1)
 
-    def pick(dest, _):
+    halo_at = tiles + dom * slot_tiles
+
+    def pick(i, _):
+        dest = (dom + i) % nd
         wanted = wanted_ref[pl.ds(dest, 1), :]
         low, high = wanted & 127, wanted >> 7
         choose = jnp.where(lane_ids == low, 1.0, 0.0).astype(BF)
@@ -130,39 +136,58 @@
         found = jnp.where(live, found, 0.0).astype(BF)
         for j in range(slot_tiles):
             halo_out[dest, j] = found[:, j * 128 : (j + 1) * 128]
-        return 0
-
-    lax.fori_loop(0, nd, pick, 0)
-    halo_at = tiles + dom * slot_tiles
+
+        @pl.when(dest != dom)
+        def _():
+            send(
+                halo_out.at[dest], ext.at[pl.ds(halo_at, slot_tiles)], 0,
+                {"feat": feat, "dom": dest},
+            )
+
+        return 0
+
+    def outward(first, count):
+        def weights_z(i, _):
+            there = (z + first + i) % nz
+
+            @pl.when(there != z)
+            def _():
+                send(my_unit, my_unit, 1, feat_at(x, there))
+
+            return 0
+
+        def features_out(i, _):
+            peer = (x + i) % nx * nz + (z + first + i // nx) % nz
+
+            @pl.when(peer != feat)
+            def _():
+                send(ext.at[peer], xm.at[0, slot], 2, {"feat": peer, "dom": dom})
+
+            return 0
+
+        lax.fori_loop(0, count, weights_z, 0)
+        lax.fori_loop(0, count * nx, features_out, 0)
+
+    if nz > 11:
+        reach = (((nz - 2, 5),), ((3, 3), (nz - 5, 3)), ((6, nz - 11),))
+    elif nz > 5:
+        reach = (((nz - 2, 5),), ((3, nz - 5),), ())
+    else:
+        reach = (((0, nz),), (), ())
+    third = nd // 3 + 1
+    pl.semaphore_wait(barrier, len(near) + nx - 1 + nd - 1)
+    for r, offsets in enumerate((near, along(3), along(5))):
+        round_out(r, offsets)
+        lax.fori_loop(r * third, min((r + 1) * third, nd), pick, 0)
+        if r == 0:
+            pltpu.make_async_copy(my_unit, my_unit, load_sem.at[7]).wait()
+            for load in loads[3:]:
+                load.wait()
+        pl.semaphore_wait(round_sem.at[r], len(offsets))
+        for first, count in reach[r]:
+            outward(first, count)
     for j in range(slot_tiles):
         ext[halo_at + j] = halo_out[dom, j]
-    pltpu.make_async_copy(my_unit, my_unit, load_sem.at[7]).wait()
-    for load in loads[3:]:
-        load.wait()
-    pl.semaphore_wait(barrier, nf - 1 + nd - 1)
-
-    def halo_send(i, _):
-        dest = (dom + i) % nd
-        send(
-            halo_out.at[dest], ext.at[pl.ds(halo_at, slot_tiles)], 0,
-            {"feat": feat, "dom": dest},
-        )
-        return 0
-
-    lax.fori_loop(1, nd, halo_send, 0)
-
-    def weights_z(i, _):
-        send(my_unit, my_unit, 1, feat_at(x, (z + i) % nz))
-        return 0
-
-    lax.fori_loop(1, nz, weights_z, 0)
-
-    def features_out(i, _):
-        peer = (feat + i) % nf
-        send(ext.at[peer], xm.at[0, slot], 2, {"feat": peer, "dom": dom})
-        return 0
-
-    lax.fori_loop(1, nf, features_out, 0)
 
     ones = jnp.ones((width, 256), BF)
 
@@ -477,6 +502,7 @@
             pltpu.SemaphoreType.DMA((19,)),
             pltpu.SemaphoreType.DMA((19,)),
             pltpu.SemaphoreType.DMA((8,)),
+            pltpu.SemaphoreType.REGULAR((3,)),
         ],
         compiler_params=pltpu.CompilerParams(
             collective_id=0, has_side_effects=True, vmem_limit_bytes=67_000_000

time: 79.5 us -> 78.6 us (0.989)
  Pallas kernels: 78.7 us -> 77.9 us
    pallas_call x1, Pallas kernels: 77.1 us -> 76.2 us  [on_device(): pl.pallas_call(layer, out_shape=shapes, in_specs=[hbm] * 9, out_specs=(vm...]
where the time goes in v5:
time: 78.6 us; the launch traced here: 78.5 us
  Pallas kernels  77.9 us (99%)
    pallas_call x1, Pallas kernels, on_device(): pl.pallas_call(layer, out_shape=shapes, in_specs=[hbm] * 9, out_specs=(vm...  76.2 us
    pallas_call x1, Pallas kernels, on_device(): pl.pallas_call(store_out, out_shape=shapes, in_specs=[hbm] * 3, out_specs...  1.63 us

profile of v5, /device:TPU:1, one launch (start us, length us, event | category | flops | bytes accessed | tf_op | source)
XLA Modules:
  0.0 78.5 jit_solution(1800362108221940527)
XLA Ops:
  0.6 76.2 %shard_map.112 = (bf16[128,512]{1,0:T(8,128)(2,1)}, f32[16,512]{1,0:T(8,128)}, f32[16,512]{1,0:T(8,128)}) custom-call(bf16[16,8192]{1,0:T(8,128)(2,1)} %bitcast.7, bf16[16,512]{1,0:T(8,128)(2,1)} %w1_hbm.1, bf16[16,512]{1,0:T(8,128)(2,1)} %w2_hbm.1, bf16[128,512]{1,0:T(8,128)(2,1)} %cot_hbm.1, s32[8,8,256]{2,1,0:T(8,128)} %rows_hbm.1, ...), custom_call_target="tpu_custom_call" | custom-call | tf_op jit(solution)/shard_map/pallas_call | solution.py:464
  76.9 1.6 %shard_map.113 = (bf16[128,512]{1,0:T(8,128)(2,1)}, f32[16,512]{1,0:T(8,128)}, f32[16,512]{1,0:T(8,128)}) custom-call(bf16[128,512]{1,0:T(8,128)(2,1)} %get-tuple-element.6.hid_in, f32[16,512]{1,0:T(8,128)} %get-tuple-element.7.gs_in, f32[16,512]{1,0:T(8,128)} %get-tuple-element.8.gn_in), custom_call_target="tpu_custom_call" | custom-call | tf_op jit(solution)/shard_map/pallas_call | solution.py:513

commit v6 on v5

--- a/solution.py
+++ b/solution.py
@@ -28,7 +28,7 @@
     x_hbm, w1_hbm, w2_hbm, cot_hbm, rows_hbm, pat_hbm, count_hbm, source_hbm, kind_hbm,
     hid_ref, gs_ref, gn_ref,
     x_own, wanted_ref, pats, cot, count_ref, source_ref, kind_ref,
-    ext, halo_out, mean, xm, weights, partial, grad, other_a, other_a_in, other_b, other_b_in,
+    ext, halo_out, mean, by_z, xm, weights, partial, grad, other_a, other_a_in, other_b, other_b_in,
     part_a, part_a_in, part_b, part_b_in, kept_a, kept_b,
     col_a, col_a_in, col_b, col_b_in, fin, cell, cell_in, final,
     sem_out, sem_in, load_sem, round_sem,
@@ -41,7 +41,6 @@
     x, z = feat // nz, feat % nz
     y, core = dom // nc, dom % nc
     half, zz = z // hz, z % hz
-    slot = half * (nx * hz) + x * hz + zz
     width = x_own.shape[0]
     depth = nx * hz * width
     band = hz * width
@@ -111,7 +110,6 @@
         return 0
 
     lax.fori_loop(0, tiles, take, 0)
-    xm[0, slot] = ext[feat]
 
     group = min(tiles, 16)
     lane_ids = lax.broadcasted_iota(jnp.int32, (128, slots), 0)
@@ -146,46 +144,48 @@
 
         return 0
 
-    def outward(first, count):
-        def weights_z(i, _):
-            there = (z + first + i) % nz
-
-            @pl.when(there != z)
-            def _():
-                send(my_unit, my_unit, 1, feat_at(x, there))
-
-            return 0
-
-        def features_out(i, _):
-            peer = (x + i) % nx * nz + (z + first + i // nx) % nz
-
-            @pl.when(peer != feat)
-            def _():
-                send(ext.at[peer], xm.at[0, slot], 2, {"feat": peer, "dom": dom})
-
-            return 0
-
-        lax.fori_loop(0, count, weights_z, 0)
-        lax.fori_loop(0, count * nx, features_out, 0)
-
-    if nz > 11:
-        reach = (((nz - 2, 5),), ((3, 3), (nz - 5, 3)), ((6, nz - 11),))
-    elif nz > 5:
-        reach = (((nz - 2, 5),), ((3, nz - 5),), ())
-    else:
-        reach = (((0, nz),), (), ())
-    third = nd // 3 + 1
+    def x_send(m, tiles_at, phase, column):
+        send(
+            tiles_at.at[pl.ds(column * nz, nz)], by_z.at[m, :, x], phase, feat_at(column, z)
+        )
+
+    def z_sends(m, tiles_at, in_phase, out_phase):
+        def keep(t, _):
+            by_z[m, t, x] = tiles_at[x * nz + t]
+            return 0
+
+        def z_send(i, _):
+            peer = (z + i) % nz
+            send(by_z.at[m, peer], xm.at[m, half, zz], out_phase, feat_at(x, peer))
+            return 0
+
+        lax.fori_loop(0, nz, keep, 0)
+        drain(tiles_at.at[pl.ds(0, (nx - 1) * nz)], sem_in.at[in_phase])
+        lax.fori_loop(1, nz, z_send, 0)
+        xm[m, half, zz] = by_z[m, z]
+
+    assert nz <= 17
     pl.semaphore_wait(barrier, len(near) + nx - 1 + nd - 1)
-    for r, offsets in enumerate((near, along(3), along(5))):
-        round_out(r, offsets)
-        lax.fori_loop(r * third, min((r + 1) * third, nd), pick, 0)
-        if r == 0:
-            pltpu.make_async_copy(my_unit, my_unit, load_sem.at[7]).wait()
-            for load in loads[3:]:
-                load.wait()
-        pl.semaphore_wait(round_sem.at[r], len(offsets))
-        for first, count in reach[r]:
-            outward(first, count)
+    round_out(0, near)
+    for i in range(1, nx):
+        x_send(0, ext, 2, (x + i) % nx)
+    lax.fori_loop(0, nd // 2, pick, 0)
+    pltpu.make_async_copy(my_unit, my_unit, load_sem.at[7]).wait()
+    pl.semaphore_wait(round_sem.at[0], len(near))
+    middle = along(4)
+    round_out(1, middle)
+    lax.fori_loop(nd // 2, nd, pick, 0)
+    for load in loads[3:]:
+        load.wait()
+    if middle:
+        pl.semaphore_wait(round_sem.at[1], len(middle))
+
+    def weights_z(i, _):
+        send(my_unit, my_unit, 1, feat_at(x, (z + i) % nz))
+        return 0
+
+    lax.fori_loop(1, nz, weights_z, 0)
+    z_sends(0, ext, 2, 19)
     for j in range(slot_tiles):
         ext[halo_at + j] = halo_out[dom, j]
 
@@ -202,22 +202,28 @@
             )
         return (total[:width] / total[width : width + 1]).astype(BF)
 
-    def mean_out(i, _):
-        peers = [(feat + 1 + 2 * i + j) % nf for j in range(2)]
-        found = [mean_of(peer) for peer in peers]
-        for peer, value in zip(peers, found):
-            mean[peer] = value
-        for peer in peers:
-
-            @pl.when(peer != feat)
-            def _():
-                send(mean.at[peer], xm.at[1, slot], 3, {"feat": peer, "dom": dom})
-
-        return 0
-
     drain(ext.at[pl.ds(tiles, (nd - 1) * slot_tiles)], sem_in.at[0])
-    lax.fori_loop(0, nf // 2, mean_out, 0)
-    xm[1, slot] = mean[feat]
+
+    def column_out(g, _):
+        column = (x + 1 + g) % nx
+
+        def mean_pair(i, _):
+            t = column * nz + 2 * i
+            first, second = mean_of(t), mean_of(t + 1)
+            mean[t] = first
+            mean[t + 1] = second
+            return 0
+
+        lax.fori_loop(0, nz // 2, mean_pair, 0)
+
+        @pl.when(column != x)
+        def _():
+            x_send(1, mean, 3, column)
+
+        return 0
+
+    lax.fori_loop(0, nx, column_out, 0)
+    z_sends(1, mean, 3, 20)
 
     drain(ext.at[pl.ds(0, nz - 1)], sem_in.at[1])
     first_a, first_b = weights.at[0, core, y, x], weights.at[1, core, y, x]
@@ -237,7 +243,7 @@
     drain(weights.at[1, core, :, pl.ds(0, nx - 1)], sem_in.at[7])
     for h in range(2):
         send(weights.at[h, core], weights.at[h, core], 8, dom_at(y, 1 - core))
-    drain(xm.at[0, pl.ds(0, nf - 1)], sem_in.at[2])
+    drain(by_z.at[0, pl.ds(0, nz - 1)], sem_in.at[19])
 
     def times_weights(m, own, b):
         total = jnp.zeros((128, 128), F32)
@@ -248,23 +254,25 @@
             )
         return total
 
+    def rows_of(m, h, b):
+        return xm[m, h, :, b].reshape(band, 128)
+
     def halves(m):
-        return [xm[m, h * nx * hz : (h + 1) * nx * hz].reshape(depth, 128) for h in range(2)]
+        return [
+            jnp.concatenate([rows_of(m, h, b) for b in range(nx)], axis=0) for h in range(2)
+        ]
 
     drain(weights.at[0], sem_in.at[8])
     own = halves(0)
     for b in range(ny):
         partial[:, b * 128 : (b + 1) * 128] = times_weights(0, own, b)
-    drain(xm.at[1, pl.ds(0, nf - 1)], sem_in.at[3])
+    drain(by_z.at[1, pl.ds(0, nz - 1)], sem_in.at[20])
     own = halves(1)
     for b in range(ny):
         span = slice(b * 128, (b + 1) * 128)
         value, slope = gelu_pair(partial[:, span] + times_weights(1, own, b))
         hid_ref[:, span] = value.astype(BF)
         grad[:, span] = (cot[:, span].astype(F32) * slope).astype(BF)
-
-    def rows_of(m, h, b):
-        return xm[m, pl.ds(h * nx * hz + b * hz, hz)].reshape(band, 128)
 
     def product_a(m, b):
         return jnp.dot(rows_of(m, 0, b), grad[...], preferred_element_type=F32)
@@ -411,15 +419,15 @@
         gn_ref[:, span] = final[b * nc + 1]
 
     sent = (
-        halo_out.at[pl.ds(0, nd - 1)], ext.at[pl.ds(0, nz - 1)], ext.at[pl.ds(0, nf - 1)],
-        mean.at[pl.ds(0, nf - 1)], weights.at[0, core, y, pl.ds(0, nx - 1)],
+        halo_out.at[pl.ds(0, nd - 1)], ext.at[pl.ds(0, nz - 1)],
+        ext.at[pl.ds(0, (nx - 1) * nz)], mean.at[pl.ds(0, (nx - 1) * nz)], weights.at[0, core, y, pl.ds(0, nx - 1)],
         weights.at[1, core, pl.ds(0, ny - 1), x], weights.at[0, core, pl.ds(0, ny - 1)],
         weights.at[1, core, :, pl.ds(0, nx - 1)], weights.at[0],
         other_a.at[pl.ds(0, nx // 2)], other_a.at[pl.ds(0, nx // 2)],
         other_b.at[pl.ds(0, ny // 2)], other_b.at[pl.ds(0, ny // 2)],
         part_a.at[pl.ds(0, ny - 1)], part_b.at[pl.ds(0, nx - 1)],
         col_a.at[pl.ds(0, nx - 1)], col_b.at[pl.ds(0, ny - 1)], cell.at[pl.ds(0, nz - 1)],
-        final.at[pl.ds(0, nd - 1)],
+        final.at[pl.ds(0, nd - 1)], by_z.at[0, pl.ds(0, nz - 1)], by_z.at[1, pl.ds(0, nz - 1)],
     )
     for phase, ref in enumerate(sent):
         drain(ref, sem_out.at[phase])
@@ -477,7 +485,8 @@
             pltpu.VMEM((nf + nd * slot_tiles, width, 128), BF),
             pltpu.VMEM((nd, slot_tiles, width, 128), BF),
             pltpu.VMEM((nf, width, 128), BF),
-            pltpu.VMEM((2, nf, width, 128), BF),
+            pltpu.VMEM((2, nz, nx, width, 128), BF),
+            pltpu.VMEM((2, 2, hz, nx, width, 128), BF),
             pltpu.VMEM((2, nc, ny, nx, hz, width, 128), BF),
             pltpu.VMEM((128, hidden), F32),
             pltpu.VMEM((128, hidden), BF),
@@ -499,10 +508,10 @@
             pltpu.VMEM((nz, width, 128), BF),
             pltpu.VMEM((nz, width, 128), BF),
             pltpu.VMEM((nd, width, 128), F32),
-            pltpu.SemaphoreType.DMA((19,)),
-            pltpu.SemaphoreType.DMA((19,)),
+            pltpu.SemaphoreType.DMA((21,)),
+            pltpu.SemaphoreType.DMA((21,)),
             pltpu.SemaphoreType.DMA((8,)),
-            pltpu.SemaphoreType.REGULAR((3,)),
+            pltpu.SemaphoreType.REGULAR((2,)),
         ],
         compiler_params=pltpu.CompilerParams(
             collective_id=0, has_side_effects=True, vmem_limit_bytes=67_000_000

time: 78.6 us -> 79.4 us (1.010)
  no operation moved by 1% of the time
where the time goes in v6:
time: 79.4 us; the launch traced here: 79.2 us
  Pallas kernels  78.6 us (99%)
    pallas_call x1, Pallas kernels, on_device(): pl.pallas_call(layer, out_shape=shapes, in_specs=[hbm] * 9, out_specs=(vm...  77 us
    pallas_call x1, Pallas kernels, on_device(): pl.pallas_call(store_out, out_shape=shapes, in_specs=[hbm] * 3, out_specs...  1.63 us

profile of v6, /device:TPU:1, one launch (start us, length us, event | category | flops | bytes accessed | tf_op | source)
XLA Modules:
  0.0 79.2 jit_solution(10760710596103208844)
XLA Ops:
  0.6 77.0 %shard_map.112 = (bf16[128,512]{1,0:T(8,128)(2,1)}, f32[16,512]{1,0:T(8,128)}, f32[16,512]{1,0:T(8,128)}) custom-call(bf16[16,8192]{1,0:T(8,128)(2,1)} %bitcast.7, bf16[16,512]{1,0:T(8,128)(2,1)} %w1_hbm.1, bf16[16,512]{1,0:T(8,128)(2,1)} %w2_hbm.1, bf16[128,512]{1,0:T(8,128)(2,1)} %cot_hbm.1, s32[8,8,256]{2,1,0:T(8,128)} %rows_hbm.1, ...), custom_call_target="tpu_custom_call" | custom-call | tf_op jit(solution)/shard_map/pallas_call | solution.py:472
  77.6 1.6 %shard_map.113 = (bf16[128,512]{1,0:T(8,128)(2,1)}, f32[16,512]{1,0:T(8,128)}, f32[16,512]{1,0:T(8,128)}) custom-call(bf16[128,512]{1,0:T(8,128)(2,1)} %get-tuple-element.6.hid_in, f32[16,512]{1,0:T(8,128)} %get-tuple-element.7.gs_in, f32[16,512]{1,0:T(8,128)} %get-tuple-element.8.gn_in), custom_call_target="tpu_custom_call" | custom-call | tf_op jit(solution)/shard_map/pallas_call | solution.py:522

commit v7 on v6

--- a/solution.py
+++ b/solution.py
@@ -144,6 +144,8 @@
 
         return 0
 
+    outward = sorted(range(1, nz), key=lambda i: (-min(i, nz - i), i))
+
     def x_send(m, tiles_at, phase, column):
         send(
             tiles_at.at[pl.ds(column * nz, nz)], by_z.at[m, :, x], phase, feat_at(column, z)
@@ -154,14 +156,11 @@
             by_z[m, t, x] = tiles_at[x * nz + t]
             return 0
 
-        def z_send(i, _):
+        lax.fori_loop(0, nz, keep, 0)
+        drain(tiles_at.at[pl.ds(0, (nx - 1) * nz)], sem_in.at[in_phase])
+        for i in outward:
             peer = (z + i) % nz
             send(by_z.at[m, peer], xm.at[m, half, zz], out_phase, feat_at(x, peer))
-            return 0
-
-        lax.fori_loop(0, nz, keep, 0)
-        drain(tiles_at.at[pl.ds(0, (nx - 1) * nz)], sem_in.at[in_phase])
-        lax.fori_loop(1, nz, z_send, 0)
         xm[m, half, zz] = by_z[m, z]
 
     assert nz <= 17
@@ -180,11 +179,8 @@
     if middle:
         pl.semaphore_wait(round_sem.at[1], len(middle))
 
-    def weights_z(i, _):
+    for i in outward:
         send(my_unit, my_unit, 1, feat_at(x, (z + i) % nz))
-        return 0
-
-    lax.fori_loop(1, nz, weights_z, 0)
     z_sends(0, ext, 2, 19)
     for j in range(slot_tiles):
         ext[halo_at + j] = halo_out[dom, j]
@@ -377,14 +373,13 @@
     lax.fori_loop(1, ny, y_then, 0)
     fin[1] = x_sum(y)
 
-    def z_out(i, _):
-        peer = i
-
-        @pl.when(peer != z)
-        def _():
-            send(cell.at[peer], cell_in.at[z], 17, feat_at(x, peer))
-
-        return 0
+    def z_out(h):
+        for i in outward:
+            peer = (z + i) % nz
+
+            @pl.when(peer // hz == h)
+            def _(peer=peer):
+                send(cell.at[peer], cell_in.at[z], 17, feat_at(x, peer))
 
     drain(col_a_in.at[pl.ds(0, nx - 1)], sem_in.at[15])
     total = fin[0]
@@ -392,14 +387,14 @@
         total = total + col_a_in[(x + j) % nx].astype(F32)
     fin[0] = total
     cell[0:hz] = total.astype(BF).reshape(hz, width, 128)
-    lax.fori_loop(0, hz, z_out, 0)
+    z_out(0)
     drain(col_b_in.at[pl.ds(0, ny - 1)], sem_in.at[16])
     total = fin[1]
     for j in range(1, ny):
         total = total + col_b_in[(y + j) % ny].astype(F32)
     fin[1] = total
     cell[hz:nz] = total.astype(BF).reshape(hz, width, 128)
-    lax.fori_loop(hz, nz, z_out, 0)
+    z_out(1)
     drain(cell_in.at[pl.ds(0, nz - 1)], sem_in.at[17])
     total = fin[half, pl.ds(pl.multiple_of(zz * width, width), width)]
     for j in range(1, nz):

time: 79.4 us -> 76.2 us (0.960)
  Pallas kernels: 78.6 us -> 75.4 us
    pallas_call x1, Pallas kernels: 77 us -> 73.8 us  [on_device(): pl.pallas_call(layer, out_shape=shapes, in_specs=[hbm] * 9, out_specs=(vm...]
where the time goes in v7:
time: 76.2 us; the launch traced here: 76.1 us
  Pallas kernels  75.4 us (99%)
    pallas_call x1, Pallas kernels, on_device(): pl.pallas_call(layer, out_shape=shapes, in_specs=[hbm] * 9, out_specs=(vm...  73.8 us
    pallas_call x1, Pallas kernels, on_device(): pl.pallas_call(store_out, out_shape=shapes, in_specs=[hbm] * 3, out_specs...  1.63 us

profile of v7, /device:TPU:1, one launch (start us, length us, event | category | flops | bytes accessed | tf_op | source)
XLA Modules:
  0.0 76.1 jit_solution(14186789584873563440)
XLA Ops:
  0.6 73.8 %shard_map.112 = (bf16[128,512]{1,0:T(8,128)(2,1)}, f32[16,512]{1,0:T(8,128)}, f32[16,512]{1,0:T(8,128)}) custom-call(bf16[16,8192]{1,0:T(8,128)(2,1)} %bitcast.7, bf16[16,512]{1,0:T(8,128)(2,1)} %w1_hbm.1, bf16[16,512]{1,0:T(8,128)(2,1)} %w2_hbm.1, bf16[128,512]{1,0:T(8,128)(2,1)} %cot_hbm.1, s32[8,8,256]{2,1,0:T(8,128)} %rows_hbm.1, ...), custom_call_target="tpu_custom_call" | custom-call | tf_op jit(solution)/shard_map/pallas_call | solution.py:467
  74.4 1.6 %shard_map.113 = (bf16[128,512]{1,0:T(8,128)(2,1)}, f32[16,512]{1,0:T(8,128)}, f32[16,512]{1,0:T(8,128)}) custom-call(bf16[128,512]{1,0:T(8,128)(2,1)} %get-tuple-element.6.hid_in, f32[16,512]{1,0:T(8,128)} %get-tuple-element.7.gs_in, f32[16,512]{1,0:T(8,128)} %get-tuple-element.8.gn_in), custom_call_target="tpu_custom_call" | custom-call | tf_op jit(solution)/shard_map/pallas_call | solution.py:517

commit v8 on v7

--- a/solution.py
+++ b/solution.py
@@ -144,44 +144,50 @@
 
         return 0
 
-    outward = sorted(range(1, nz), key=lambda i: (-min(i, nz - i), i))
-
-    def x_send(m, tiles_at, phase, column):
+    def ring(n):
+        return sorted(range(1, n), key=lambda i: (-min(i, n - i), i))
+
+    outward = ring(nz)
+
+    def x_send(m, tiles_at, phase, i):
+        column = (x + i) % nx
         send(
-            tiles_at.at[pl.ds(column * nz, nz)], by_z.at[m, :, x], phase, feat_at(column, z)
+            tiles_at.at[pl.ds(column * nz, nz)], by_z.at[m, :, nx - i], phase, feat_at(column, z)
         )
 
-    def z_sends(m, tiles_at, in_phase, out_phase):
-        def keep(t, _):
-            by_z[m, t, x] = tiles_at[x * nz + t]
-            return 0
-
-        lax.fori_loop(0, nz, keep, 0)
-        drain(tiles_at.at[pl.ds(0, (nx - 1) * nz)], sem_in.at[in_phase])
+    def z_first(least, most):
         for i in outward:
-            peer = (z + i) % nz
-            send(by_z.at[m, peer], xm.at[m, half, zz], out_phase, feat_at(x, peer))
-        xm[m, half, zz] = by_z[m, z]
+            if least < min(i, nz - i) <= most:
+                peer = (z + i) % nz
+                send(my_unit, my_unit, 1, feat_at(x, peer))
+                send(ext.at[x * nz + peer], xm.at[0, half, zz, 0], 21, feat_at(x, peer))
 
     assert nz <= 17
+    pltpu.make_async_copy(my_unit, my_unit, load_sem.at[7]).wait()
     pl.semaphore_wait(barrier, len(near) + nx - 1 + nd - 1)
     round_out(0, near)
-    for i in range(1, nx):
-        x_send(0, ext, 2, (x + i) % nx)
+    for i in ring(nx):
+        x_send(0, ext, 2, i)
+    z_first(0, 2)
     lax.fori_loop(0, nd // 2, pick, 0)
-    pltpu.make_async_copy(my_unit, my_unit, load_sem.at[7]).wait()
     pl.semaphore_wait(round_sem.at[0], len(near))
     middle = along(4)
     round_out(1, middle)
+    z_first(2, 4)
     lax.fori_loop(nd // 2, nd, pick, 0)
     for load in loads[3:]:
         load.wait()
     if middle:
         pl.semaphore_wait(round_sem.at[1], len(middle))
-
+    z_first(4, nz)
+    xm[0, half, zz, 0] = ext[feat]
+    drain(ext.at[pl.ds(0, (nx - 1) * nz)], sem_in.at[2])
+    others = pl.ds(1, nx - 1)
     for i in outward:
-        send(my_unit, my_unit, 1, feat_at(x, (z + i) % nz))
-    z_sends(0, ext, 2, 19)
+        peer = (z + i) % nz
+        send(by_z.at[0, peer, others], xm.at[0, half, zz, others], 19, feat_at(x, peer))
+    for j in range(1, nx):
+        xm[0, half, zz, j] = by_z[0, z, j]
     for j in range(slot_tiles):
         ext[halo_at + j] = halo_out[dom, j]
 
@@ -200,9 +206,7 @@
 
     drain(ext.at[pl.ds(tiles, (nd - 1) * slot_tiles)], sem_in.at[0])
 
-    def column_out(g, _):
-        column = (x + 1 + g) % nx
-
+    def column_means(column):
         def mean_pair(i, _):
             t = column * nz + 2 * i
             first, second = mean_of(t), mean_of(t + 1)
@@ -212,34 +216,45 @@
 
         lax.fori_loop(0, nz // 2, mean_pair, 0)
 
-        @pl.when(column != x)
-        def _():
-            x_send(1, mean, 3, column)
-
-        return 0
-
-    lax.fori_loop(0, nx, column_out, 0)
-    z_sends(1, mean, 3, 20)
+    def column_out(i, _):
+        column_means((x + i) % nx)
+        x_send(1, mean, 3, i)
+        return 0
+
+    lax.fori_loop(1, nx, column_out, 0)
+    column_means(x)
+
+    def keep(t, _):
+        by_z[1, t, 0] = mean[x * nz + t]
+        return 0
+
+    lax.fori_loop(0, nz, keep, 0)
+    drain(mean.at[pl.ds(0, (nx - 1) * nz)], sem_in.at[3])
+    for i in outward:
+        peer = (z + i) % nz
+        send(by_z.at[1, peer], xm.at[1, half, zz], 20, feat_at(x, peer))
+    xm[1, half, zz] = by_z[1, z]
 
     drain(ext.at[pl.ds(0, nz - 1)], sem_in.at[1])
     first_a, first_b = weights.at[0, core, y, x], weights.at[1, core, y, x]
-    for i in range(1, nx):
+    for i in ring(nx):
         send(first_a, first_a, 4, feat_at((x + i) % nx, z))
-    for i in range(1, ny):
+    for i in ring(ny):
         send(first_b, first_b, 5, dom_at((y + i) % ny, core))
     drain(weights.at[0, core, y, pl.ds(0, nx - 1)], sem_in.at[4])
     then_a = weights.at[0, core, y]
-    for i in range(1, ny):
+    for i in ring(ny):
         send(then_a, then_a, 6, dom_at((y + i) % ny, core))
     drain(weights.at[1, core, pl.ds(0, ny - 1), x], sem_in.at[5])
     then_b = weights.at[1, core, :, x]
-    for i in range(1, nx):
+    for i in ring(nx):
         send(then_b, then_b, 7, feat_at((x + i) % nx, z))
     drain(weights.at[0, core, pl.ds(0, ny - 1)], sem_in.at[6])
     drain(weights.at[1, core, :, pl.ds(0, nx - 1)], sem_in.at[7])
     for h in range(2):
         send(weights.at[h, core], weights.at[h, core], 8, dom_at(y, 1 - core))
-    drain(by_z.at[0, pl.ds(0, nz - 1)], sem_in.at[19])
+    drain(by_z.at[0, pl.ds(0, nz - 1), pl.ds(1, nx - 1)], sem_in.at[19])
+    drain(ext.at[pl.ds(0, nz - 1)], sem_in.at[21])
 
     def times_weights(m, own, b):
         total = jnp.zeros((128, 128), F32)
@@ -251,7 +266,7 @@
         return total
 
     def rows_of(m, h, b):
-        return xm[m, h, :, b].reshape(band, 128)
+        return xm[m, h, :, (b + nx - x) % nx].reshape(band, 128)
 
     def halves(m):
         return [
@@ -329,13 +344,13 @@
         piece = pl.ds(p * ca, ca)
         drain(other_a_in.at[piece], sem_in.at[9 + p])
         lax.fori_loop(p * ca, (p + 1) * ca, y_first, 0)
-        for i in range(1, ny):
+        for i in ring(ny):
             c = (y + i) % ny
             send(part_a.at[c, piece], part_a_in.at[y, piece], 13, dom_at(c, core))
         piece = pl.ds(p * cb, cb)
         drain(other_b_in.at[piece], sem_in.at[11 + p])
         lax.fori_loop(0, nx, x_first, 0)
-        for i in range(1, nx):
+        for i in ring(nx):
             b = (x + i) % nx
             send(part_b.at[b, piece], part_b_in.at[x, piece], 14, feat_at(b, z))
 
@@ -422,7 +437,8 @@
         other_b.at[pl.ds(0, ny // 2)], other_b.at[pl.ds(0, ny // 2)],
         part_a.at[pl.ds(0, ny - 1)], part_b.at[pl.ds(0, nx - 1)],
         col_a.at[pl.ds(0, nx - 1)], col_b.at[pl.ds(0, ny - 1)], cell.at[pl.ds(0, nz - 1)],
-        final.at[pl.ds(0, nd - 1)], by_z.at[0, pl.ds(0, nz - 1)], by_z.at[1, pl.ds(0, nz - 1)],
+        final.at[pl.ds(0, nd - 1)], by_z.at[0, pl.ds(0, nz - 1), pl.ds(1, nx - 1)],
+        by_z.at[1, pl.ds(0, nz - 1)], ext.at[pl.ds(0, nz - 1)],
     )
     for phase, ref in enumerate(sent):
         drain(ref, sem_out.at[phase])
@@ -503,8 +519,8 @@
             pltpu.VMEM((nz, width, 128), BF),
             pltpu.VMEM((nz, width, 128), BF),
             pltpu.VMEM((nd, width, 128), F32),
-            pltpu.SemaphoreType.DMA((21,)),
-            pltpu.SemaphoreType.DMA((21,)),
+            pltpu.SemaphoreType.DMA((22,)),
+            pltpu.SemaphoreType.DMA((22,)),
             pltpu.SemaphoreType.DMA((8,)),
             pltpu.SemaphoreType.REGULAR((2,)),
         ],

time: 76.2 us -> 74.5 us (0.978)
  Pallas kernels: 75.4 us -> 73.7 us
    pallas_call x1, Pallas kernels: 73.8 us -> 72.1 us  [on_device(): pl.pallas_call(layer, out_shape=shapes, in_specs=[hbm] * 9, out_specs=(vm...]
where the time goes in v8:
time: 74.5 us; the launch traced here: 74.3 us
  Pallas kernels  73.7 us (99%)
    pallas_call x1, Pallas kernels, on_device(): pl.pallas_call(layer, out_shape=shapes, in_specs=[hbm] * 9, out_specs=(vm...  72.1 us
    pallas_call x1, Pallas kernels, on_device(): pl.pallas_call(store_out, out_shape=shapes, in_specs=[hbm] * 3, out_specs...  1.63 us

profile of v8, /device:TPU:1, one launch (start us, length us, event | category | flops | bytes accessed | tf_op | source)
XLA Modules:
  0.0 74.3 jit_solution(5887049482618328607)
XLA Ops:
  0.6 72.1 %shard_map.112 = (bf16[128,512]{1,0:T(8,128)(2,1)}, f32[16,512]{1,0:T(8,128)}, f32[16,512]{1,0:T(8,128)}) custom-call(bf16[16,8192]{1,0:T(8,128)(2,1)} %bitcast.7, bf16[16,512]{1,0:T(8,128)(2,1)} %w1_hbm.1, bf16[16,512]{1,0:T(8,128)(2,1)} %w2_hbm.1, bf16[128,512]{1,0:T(8,128)(2,1)} %cot_hbm.1, s32[8,8,256]{2,1,0:T(8,128)} %rows_hbm.1, ...), custom_call_target="tpu_custom_call" | custom-call | tf_op jit(solution)/shard_map/pallas_call | solution.py:483
  72.7 1.6 %shard_map.113 = (bf16[128,512]{1,0:T(8,128)(2,1)}, f32[16,512]{1,0:T(8,128)}, f32[16,512]{1,0:T(8,128)}) custom-call(bf16[128,512]{1,0:T(8,128)(2,1)} %get-tuple-element.6.hid_in, f32[16,512]{1,0:T(8,128)} %get-tuple-element.7.gs_in, f32[16,512]{1,0:T(8,128)} %get-tuple-element.8.gn_in), custom_call_target="tpu_custom_call" | custom-call | tf_op jit(solution)/shard_map/pallas_call | solution.py:533

commit v9 on v8

--- a/solution.py
+++ b/solution.py
@@ -229,18 +229,18 @@
         return 0
 
     lax.fori_loop(0, nz, keep, 0)
-    drain(mean.at[pl.ds(0, (nx - 1) * nz)], sem_in.at[3])
-    for i in outward:
-        peer = (z + i) % nz
-        send(by_z.at[1, peer], xm.at[1, half, zz], 20, feat_at(x, peer))
-    xm[1, half, zz] = by_z[1, z]
-
     drain(ext.at[pl.ds(0, nz - 1)], sem_in.at[1])
     first_a, first_b = weights.at[0, core, y, x], weights.at[1, core, y, x]
     for i in ring(nx):
         send(first_a, first_a, 4, feat_at((x + i) % nx, z))
     for i in ring(ny):
         send(first_b, first_b, 5, dom_at((y + i) % ny, core))
+    drain(mean.at[pl.ds(0, (nx - 1) * nz)], sem_in.at[3])
+    for i in outward:
+        peer = (z + i) % nz
+        send(by_z.at[1, peer], xm.at[1, half, zz], 20, feat_at(x, peer))
+    xm[1, half, zz] = by_z[1, z]
+
     drain(weights.at[0, core, y, pl.ds(0, nx - 1)], sem_in.at[4])
     then_a = weights.at[0, core, y]
     for i in ring(ny):

time: 74.5 us -> 74.2 us (level)
  no operation moved by 1% of the time
where the time goes in v9:
time: 74.2 us; the launch traced here: 74 us
  Pallas kernels  73.4 us (99%)
    pallas_call x1, Pallas kernels, on_device(): pl.pallas_call(layer, out_shape=shapes, in_specs=[hbm] * 9, out_specs=(vm...  71.8 us
    pallas_call x1, Pallas kernels, on_device(): pl.pallas_call(store_out, out_shape=shapes, in_specs=[hbm] * 3, out_specs...  1.63 us

profile of v9, /device:TPU:1, one launch (start us, length us, event | category | flops | bytes accessed | tf_op | source)
XLA Modules:
  0.0 74.0 jit_solution(6503459590881084726)
XLA Ops:
  0.6 71.8 %shard_map.112 = (bf16[128,512]{1,0:T(8,128)(2,1)}, f32[16,512]{1,0:T(8,128)}, f32[16,512]{1,0:T(8,128)}) custom-call(bf16[16,8192]{1,0:T(8,128)(2,1)} %bitcast.7, bf16[16,512]{1,0:T(8,128)(2,1)} %w1_hbm.1, bf16[16,512]{1,0:T(8,128)(2,1)} %w2_hbm.1, bf16[128,512]{1,0:T(8,128)(2,1)} %cot_hbm.1, s32[8,8,256]{2,1,0:T(8,128)} %rows_hbm.1, ...), custom_call_target="tpu_custom_call" | custom-call | tf_op jit(solution)/shard_map/pallas_call | solution.py:483
  72.4 1.6 %shard_map.113 = (bf16[128,512]{1,0:T(8,128)(2,1)}, f32[16,512]{1,0:T(8,128)}, f32[16,512]{1,0:T(8,128)}) custom-call(bf16[128,512]{1,0:T(8,128)(2,1)} %get-tuple-element.6.hid_in, f32[16,512]{1,0:T(8,128)} %get-tuple-element.7.gs_in, f32[16,512]{1,0:T(8,128)} %get-tuple-element.8.gn_in), custom_call_target="tpu_custom_call" | custom-call | tf_op jit(solution)/shard_map/pallas_call | solution.py:533
